TPU v7x, 32 devices: a whole 2x2x4 slice. The times are simulated.
32 devices in a mesh: grp: 2 (over x), beam: 16 (over z, y, core).
Axes of the slice: x: 2, y: 2, z: 4, core: 2. Of those that a mesh axis runs over, the one named last changes fastest.
Arguments:
- hidden: bfloat16 [3, 64, 8192], P(None, ('grp', 'beam')), parts along dimension 1, may hold values from -6 to 6
- norm_gain: float32 [8192], replicated, may hold values from 0.5 to 1.5
- q_weight: bfloat16 [8192, 8192], P(None, 'beam'), may hold values from -0.0625 to 0.0625
- q_bias: float32 [8192], P('beam'), may hold values from -3 to 3
- kv_weight: bfloat16 [8192, 2, 1024], P(None, None, 'beam'), may hold values from -0.0625 to 0.0625
- kv_bias: float32 [2, 1024], P(None, 'beam'), may hold values from -5 to 5
- o_weight: bfloat16 [8192, 8192], P(None, 'beam'), may hold values from -0.0625 to 0.0625
- prefix_key_cache: bfloat16 [8, 2048, 1024], P('grp', 'beam'), parts along dimension 0, may hold values from -100 to 100
- prefix_value_cache: bfloat16 [8, 2048, 1024], P('grp', 'beam'), parts along dimension 0, may hold values from -12 to 12
- prefix_index: int32 [4], P('grp'), parts along dimension 0, may hold values from 0 to 3
- prefix_lens: int32 [4], P('grp'), parts along dimension 0, may hold values from 8 to 2048, as said below
- tail_key_cache: bfloat16 [64, 256, 1024], P(('grp', 'beam')), parts along dimension 0, may hold values from -12 to 12
- tail_value_cache: bfloat16 [64, 256, 1024], P(('grp', 'beam')), parts along dimension 0, may hold values from -12 to 12
- tail_lens: int32 [64], P('grp'), parts along dimension 0, may hold values from 1 to 256, as said below
- parents: int32 [3, 64], P(None, 'grp'), parts along dimension 1, may hold values from 0 to 31, as said below
Outputs:
- out: bfloat16 [3, 64, 8192], P(None, 'grp', 'beam'), parts along dimension 1
There are 2 independent parts, one for each index of `grp`. A program takes and returns all parts, laid end to end along the dimension named above; an argument that names none is the same for every part. Nothing has to cross between parts.
Inputs may be any that keep to these rules, and one draw needn't show every extreme that they name: `prefix_lens`: the shared prefix lengths; some prompt uses all 2048 positions. `tail_lens`: the tail lengths; some row fills all 256 positions. parents[t, r] is one of the 16 rows of r's prompt: from r - r % 16 to r - r % 16 + 15.
All inputs are finite; a program needn't handle non-finite values.
Results may differ from a plain program's by a relative error of at most 0.012.
The roundings to bfloat16 on the way count: a program that leaves them out, or rounds other values in their place, can miss the bound.
Values may be sent and summed in bfloat16 or wider, within the bound.
A program may use at most 192 MiB of HBM per device.

v0:
```python
import math

import jax
import jax.numpy as jnp
import numpy as np
from jax import lax
from jax.sharding import PartitionSpec as P

QUERY_HEADS = 64
KEY_HEADS = 8
HEAD_DIM = 128
BEAM_COUNT = 16
STEPS = 3


EPS = 1e-06
NEG = -1e30
ROPE_BASE = 1000000.0


def rope_parts(positions, head_size):
    half = head_size // 2
    freqs = np.power(ROPE_BASE, -np.arange(half) * 2.0 / head_size)
    angle = positions.astype(jnp.float32)[:, None] * jnp.asarray(freqs, jnp.float32)[None, :]
    return (jnp.cos(angle), jnp.sin(angle))


def apply_rotation(value_rows, cosine_table, sine_table):
    half = value_rows.shape[-1] // 2
    first = value_rows[..., :half]
    second = value_rows[..., half:]
    cosine_table = cosine_table[:, None, :]
    sine_table = sine_table[:, None, :]
    return jnp.concatenate(
        [first * cosine_table - second * sine_table, second * cosine_table + first * sine_table],
        axis=-1,
    )


def local(
    hidden,
    norm_gain,
    q_weight,
    q_bias,
    kv_weight,
    kv_bias,
    o_weight,
    prefix_key_cache,
    prefix_value_cache,
    prefix_index,
    prefix_lens,
    tail_key_cache,
    tail_value_cache,
    tail_lens,
    parents,
):
    devices = lax.axis_size("beam")
    me = lax.axis_index("beam")
    rows_per_chip = hidden.shape[1]
    width = hidden.shape[2]
    all_rows = rows_per_chip * devices
    prompt_batch = all_rows // BEAM_COUNT
    head_group = QUERY_HEADS // KEY_HEADS
    q_width = QUERY_HEADS * HEAD_DIM
    q_cols = q_weight.shape[1]
    kv_cols = kv_weight.shape[2]
    prefix_slice = prefix_key_cache.shape[1]
    tail_cache = tail_key_cache.shape[1]
    score_scale = 1.0 / math.sqrt(HEAD_DIM)
    row_ids = jnp.arange(all_rows, dtype=jnp.int32)
    prompt_of = row_ids // BEAM_COUNT
    first_row = me * rows_per_chip
    my_prompt = first_row // BEAM_COUNT
    slot_ids = first_row + jnp.arange(rows_per_chip, dtype=jnp.int32)
    mine = (jnp.arange(prompt_batch, dtype=jnp.int32) == my_prompt)[:, None, None, None]
    joint = jnp.concatenate([q_weight, kv_weight.reshape(width, 2 * kv_cols)], axis=1)
    joint_bias = jnp.concatenate([q_bias, kv_bias.reshape(2 * kv_cols)])
    slice_keys = jnp.take(prefix_key_cache, prefix_index, axis=0).reshape(
        prompt_batch, prefix_slice, KEY_HEADS, HEAD_DIM
    )
    slice_values = jnp.take(prefix_value_cache, prefix_index, axis=0).reshape(
        prompt_batch, prefix_slice, KEY_HEADS, HEAD_DIM
    )
    slab_ok = (me * prefix_slice + jnp.arange(prefix_slice, dtype=jnp.int32))[
        None, :
    ] < prefix_lens[:, None]
    slab_ok = slab_ok[:, None, None, None, :]
    tail_key_rows = tail_key_cache.reshape(rows_per_chip, tail_cache, KEY_HEADS, HEAD_DIM)
    tail_value_rows = tail_value_cache.reshape(rows_per_chip, tail_cache, KEY_HEADS, HEAD_DIM)
    own_lens = lax.dynamic_slice_in_dim(tail_lens, first_row, rows_per_chip, 0)
    tail_ok = jnp.arange(tail_cache, dtype=jnp.int32)[None, :] < own_lens[:, None]
    ancestors = row_ids
    makers = []
    fresh_keys = []
    current_values = []
    results = []
    for step in range(STEPS):
        chosen = parents[step]
        ancestors = ancestors[chosen]
        makers = [item[chosen] for item in makers] + [row_ids]
        value_rows = lax.all_gather(hidden[step], "beam", axis=0, tiled=True).astype(jnp.float32)
        normed = (
            value_rows
            * lax.rsqrt(jnp.mean(value_rows * value_rows, axis=-1, keepdims=True) + EPS)
            * norm_gain
        ).astype(jnp.bfloat16)
        projected = jnp.dot(normed, joint, preferred_element_type=jnp.float32) + joint_bias
        q_part = projected[:, :q_cols].astype(jnp.bfloat16)
        kv_part = projected[:, q_cols:].astype(jnp.bfloat16).reshape(all_rows, 2, kv_cols)
        positions = prefix_lens[prompt_of] + tail_lens[ancestors] + step
        cosine_table, sine_table = rope_parts(positions, HEAD_DIM)
        q_full, kv_full = (
            lax.all_gather(q_part[:, None, :], "beam", axis=2, tiled=True),
            lax.all_gather(kv_part, "beam", axis=2, tiled=True),
        )
        q_all = q_full[:, 0, :]
        owned_key_value = lax.dynamic_slice_in_dim(kv_full, first_row, rows_per_chip, 0)
        rotated_rows = apply_rotation(
            q_all.astype(jnp.float32).reshape(all_rows, QUERY_HEADS, HEAD_DIM),
            cosine_table,
            sine_table,
        ).astype(jnp.bfloat16)
        local_cosine = lax.dynamic_slice_in_dim(cosine_table, first_row, rows_per_chip, 0)
        local_sine = lax.dynamic_slice_in_dim(sine_table, first_row, rows_per_chip, 0)
        new_key = apply_rotation(
            owned_key_value[:, 0].astype(jnp.float32).reshape(rows_per_chip, KEY_HEADS, HEAD_DIM),
            local_cosine,
            local_sine,
        ).astype(jnp.bfloat16)
        fresh_keys.append(new_key)
        current_values.append(owned_key_value[:, 1].reshape(rows_per_chip, KEY_HEADS, HEAD_DIM))
        query_rows = rotated_rows.reshape(prompt_batch, BEAM_COUNT, KEY_HEADS, head_group, HEAD_DIM)
        pre_scores = (
            jnp.einsum(
                "pbkgd,pskd->pbkgs", query_rows, slice_keys, preferred_element_type=jnp.float32
            )
            * score_scale
        )
        pre_scores = jnp.where(slab_ok, pre_scores, NEG)
        local_q = lax.dynamic_index_in_dim(query_rows, my_prompt, 0, keepdims=False)
        local_anc = lax.dynamic_slice_in_dim(ancestors, my_prompt * BEAM_COUNT, BEAM_COUNT, 0)
        t_scores = (
            jnp.einsum(
                "bkgd,itkd->bkgit", local_q, tail_key_rows, preferred_element_type=jnp.float32
            )
            * score_scale
        )
        t_valid = (local_anc[:, None] == slot_ids[None, :])[:, None, None, :, None] & tail_ok[
            None, None, None, :, :
        ]
        t_scores = jnp.where(t_valid, t_scores, NEG)
        f_keys = jnp.stack(fresh_keys, 0)
        f_values = jnp.stack(current_values, 0)
        local_made = jnp.stack(
            [
                lax.dynamic_slice_in_dim(item, my_prompt * BEAM_COUNT, BEAM_COUNT, 0)
                for item in makers
            ],
            1,
        )
        f_valid = (local_made[:, :, None] == slot_ids[None, None, :])[:, None, None, :, :]
        f_scores = (
            jnp.einsum("bkgd,jikd->bkgji", local_q, f_keys, preferred_element_type=jnp.float32)
            * score_scale
        )
        f_scores = jnp.where(f_valid, f_scores, NEG)
        local_max = jnp.maximum(t_scores.max(axis=(3, 4)), f_scores.max(axis=(3, 4)))
        pre_max = pre_scores.max(-1)
        group_maximum = jnp.where(mine, jnp.maximum(pre_max, local_max[None]), pre_max)
        mine_max = lax.dynamic_index_in_dim(group_maximum, my_prompt, 0, keepdims=False)
        pre_w = jnp.where(slab_ok, jnp.exp(pre_scores - group_maximum[..., None]), 0.0)
        totals = pre_w.sum(-1)
        numer = jnp.einsum(
            "pbkgs,pskd->pbkgd",
            pre_w.astype(jnp.bfloat16),
            slice_values,
            preferred_element_type=jnp.float32,
        )
        t_w = jnp.where(t_valid, jnp.exp(t_scores - mine_max[..., None, None]), 0.0)
        f_w = jnp.where(f_valid, jnp.exp(f_scores - mine_max[..., None, None]), 0.0)
        local_total = t_w.sum(axis=(3, 4)) + f_w.sum(axis=(3, 4))
        local_num = jnp.einsum(
            "bkgit,itkd->bkgd",
            t_w.astype(jnp.bfloat16),
            tail_value_rows,
            preferred_element_type=jnp.float32,
        )
        local_num = local_num + jnp.einsum(
            "bkgji,jikd->bkgd",
            f_w.astype(jnp.bfloat16),
            f_values,
            preferred_element_type=jnp.float32,
        )
        totals = jnp.where(mine, totals + local_total[None], totals)
        numer = jnp.where(mine[..., None], numer + local_num[None], numer)
        sending = numer.astype(jnp.bfloat16).reshape(devices, rows_per_chip, q_width)
        parts = lax.all_to_all(sending, "beam", split_axis=0, concat_axis=0, tiled=True)
        maxima, sums = (
            lax.all_to_all(
                group_maximum.reshape(devices, rows_per_chip, QUERY_HEADS),
                "beam",
                split_axis=0,
                concat_axis=0,
                tiled=True,
            ),
            lax.all_to_all(
                totals.reshape(devices, rows_per_chip, QUERY_HEADS),
                "beam",
                split_axis=0,
                concat_axis=0,
                tiled=True,
            ),
        )
        top = maxima.max(0)
        factors = jnp.exp(maxima - top[None])
        denom = (factors * sums).sum(0)
        combined = jnp.einsum(
            "srh,srhd->rhd",
            factors,
            parts.reshape(devices, rows_per_chip, QUERY_HEADS, HEAD_DIM),
            preferred_element_type=jnp.float32,
        )
        attention = (
            (combined / denom[..., None]).reshape(rows_per_chip, q_width).astype(jnp.bfloat16)
        )
        out_cols = jnp.dot(
            lax.all_gather(attention, "beam", axis=0, tiled=True),
            o_weight,
            preferred_element_type=jnp.float32,
        )
        results.append(out_cols.astype(jnp.bfloat16))
    return jnp.stack(results, 0)


def solution(mesh):
    return jax.shard_map(
        local,
        mesh=mesh,
        in_specs=(
            P(None, ("grp", "beam"), None),
            P(),
            P(None, "beam"),
            P("beam"),
            P(None, None, "beam"),
            P(None, "beam"),
            P(None, "beam"),
            P("grp", "beam", None),
            P("grp", "beam", None),
            P("grp"),
            P("grp"),
            P(("grp", "beam"), None, None),
            P(("grp", "beam"), None, None),
            P("grp"),
            P(None, "grp"),
        ),
        out_specs=P(None, "grp", "beam"),
        check_vma=False,
    )
```

profile of v0, /device:TPU:0, one launch (start us, length us, event | category | flops | bytes accessed | tf_op | source)
XLA Modules:
  0.0 525.1 jit_solution(3765944253029504411)
XLA Ops:
  7.0 26.3 %all-gather = bf16[1,32,8192]{2,0,1:T(2,128)(2,1)S(1)} all-gather(bf16[1,2,8192]{2,0,1:T(2,128)(2,1)S(1)} %copy.473), channel_id=2, replica_groups=mesh['grp'=2,'beam'=16] {'beam'}, dimensions={1}, use_global_device_ids=true | all-gather | bytes 557056 | tf_op jit(solution)/shard_map/all_gather | solution.py:101
  39.1 5.9 %fusion.35 = bf16[32,640]{1,0:T(8,128)(2,1)S(1)} fusion(bf16[8192,128]{1,0:T(8,128)(2,1)} %copy.303, bf16[8192,512]{1,0:T(8,128)(2,1)} %param.22, f32[1,32,8192]{2,0,1:T(1,128)S(1)} %convert_element_type.229, f32[8192]{0:T(1024)S(1)} %copy-done.82, f32[32]{0:T(128)S(1)} %add_rsqrt_fusion.2, f32[640]{0:T(1024)S(1)} %pad_maximum_fusion.17), kind=kOutput, calls=%fused_computation.77 | convolution fusion | flops 357343232 | bytes 11610752 | tf_op jit(solution)/shard_map/dot_general | solution.py:107
  45.2 20.6 %all-gather.4 = bf16[1,32,8192]{2,0,1:T(2,128)(2,1)S(1)} all-gather(bf16[1,2,8192]{2,0,1:T(2,128)(2,1)S(1)} %copy.481), channel_id=6, replica_groups=mesh['grp'=2,'beam'=16] {'beam'}, dimensions={1}, use_global_device_ids=true | all-gather | bytes 557056 | tf_op jit(solution)/shard_map/all_gather | solution.py:101
  68.6 24.3 %all-gather.2 = bf16[1,32,8192]{2,0,1:T(2,128)(2,1)S(1)} all-gather(bf16[1,2,8192]{2,0,1:T(2,128)(2,1)S(1)} %copy.477), channel_id=4, replica_groups=mesh['grp'=2,'beam'=16] {'beam'}, dimensions={1}, use_global_device_ids=true | all-gather | bytes 557056 | tf_op jit(solution)/shard_map/all_gather | solution.py:101
  107.7 18.9 %all-gather.3 = bf16[32,8192]{1,0:T(8,128)(2,1)S(1)} all-gather(bf16[32,512]{1,0:T(8,128)(2,1)S(1)} %slice-done.5), channel_id=5, replica_groups=mesh['grp'=2,'beam'=16] {'beam'}, dimensions={1}, use_global_device_ids=true | all-gather | bytes 557056 | tf_op jit(solution)/shard_map/all_gather | solution.py:113
  126.6 20.8 %all-gather.1 = bf16[32,8192]{1,0:T(8,128)(2,1)S(1)} all-gather(bf16[32,512]{1,0:T(8,128)(2,1)S(1)} %slice-done.3), channel_id=3, replica_groups=mesh['grp'=2,'beam'=16] {'beam'}, dimensions={1}, use_global_device_ids=true | all-gather | bytes 557056 | tf_op jit(solution)/shard_map/all_gather | solution.py:113
  156.4 18.9 %all-gather.5 = bf16[32,8192]{1,0:T(8,128)(2,1)S(1)} all-gather(bf16[32,512]{1,0:T(8,128)(2,1)S(1)} %slice-done.1), channel_id=7, replica_groups=mesh['grp'=2,'beam'=16] {'beam'}, dimensions={1}, use_global_device_ids=true | all-gather | bytes 557056 | tf_op jit(solution)/shard_map/all_gather | solution.py:113
  187.4 20.3 %all_gather.38 = bf16[32,2,1024]{0,1,2:T(2,128)(2,1)S(1)} all-gather(bf16[32,2,64]{0,1,2:T(2,128)(2,1)S(1)} %copy.312), channel_id=1, replica_groups=mesh['grp'=2,'beam'=16] {'beam'}, dimensions={2}, use_global_device_ids=true | all-gather | bytes 139264 | tf_op jit(solution)/shard_map/all_gather | solution.py:114
  207.7 18.9 %all_gather.46 = bf16[32,2,1024]{0,1,2:T(2,128)(2,1)S(1)} all-gather(bf16[32,2,64]{0,1,2:T(2,128)(2,1)S(1)} %copy.368), channel_id=1, replica_groups=mesh['grp'=2,'beam'=16] {'beam'}, dimensions={2}, use_global_device_ids=true | all-gather | bytes 139264 | tf_op jit(solution)/shard_map/all_gather | solution.py:114
  226.5 20.5 %all_gather.42 = bf16[32,2,1024]{0,1,2:T(2,128)(2,1)S(1)} all-gather(bf16[32,2,64]{0,1,2:T(2,128)(2,1)} %copy.339), channel_id=1, replica_groups=mesh['grp'=2,'beam'=16] {'beam'}, dimensions={2}, use_global_device_ids=true | all-gather | bytes 139264 | tf_op jit(solution)/shard_map/all_gather | solution.py:114
  357.1 4.3 all-to-all-start.5
  367.8 4.5 all-to-all-start.3
  378.7 4.2 all-to-all-start.2
  389.4 5.8 %all-to-all-start.1 = ((bf16[16,2,8192]{2,1,0:T(2,128)(2,1)}), bf16[16,2,8192]{2,1,0:T(2,128)(2,1)}, u32[]{:S(2)}, u32[]{:S(2)}) async-start(bf16[16,2,8192]{2,1,0:T(2,128)(2,1)} %reshape.830), calls=%async_computation.1 | async-start | bytes 1048576 | tf_op jit(solution)/shard_map/all_to_all | solution.py:197
  409.7 4.1 all-to-all-start.4
  421.4 6.8 %all-to-all-done.4 = bf16[16,2,8192]{2,1,0:T(2,128)(2,1)S(1)} async-done(((bf16[16,2,8192]{2,1,0:T(2,128)(2,1)}), bf16[16,2,8192]{2,1,0:T(2,128)(2,1)S(1)}, u32[]{:S(2)}, u32[]{:S(2)}) %all-to-all-start.4) | async-done | bytes 524320 | tf_op jit(solution)/shard_map/all_to_all | solution.py:197
  428.3 4.4 all-to-all-start.7
  435.9 11.1 %all-to-all-done.7 = bf16[16,2,8192]{2,1,0:T(2,128)(2,1)S(1)} async-done(((bf16[16,2,8192]{2,1,0:T(2,128)(2,1)}), bf16[16,2,8192]{2,1,0:T(2,128)(2,1)S(1)}, u32[]{:S(2)}, u32[]{:S(2)}) %all-to-all-start.7) | async-done | bytes 524320 | tf_op jit(solution)/shard_map/all_to_all | solution.py:197
  448.0 21.3 %all-gather.8 = bf16[16,2,8192]{2,1,0:T(2,128)(2,1)S(1)} all-gather(bf16[1,2,8192]{2,1,0:T(2,128)(2,1)S(1)} %reshape.969), channel_id=1, replica_groups=mesh['grp'=2,'beam'=16] {'beam'}, dimensions={0}, use_global_device_ids=true | all-gather | bytes 557056 | tf_op jit(solution)/shard_map/all_gather | solution.py:227
  469.5 18.9 %all-gather.7 = bf16[16,2,8192]{2,1,0:T(2,128)(2,1)S(1)} all-gather(bf16[1,2,8192]{2,1,0:T(2,128)(2,1)S(1)} %reshape.967), channel_id=1, replica_groups=mesh['grp'=2,'beam'=16] {'beam'}, dimensions={0}, use_global_device_ids=true | all-gather | bytes 557056 | tf_op jit(solution)/shard_map/all_gather | solution.py:227
  488.6 4.9 fusion.38
  493.5 4.9 fusion.37
  498.4 20.3 %all-gather.6 = bf16[16,2,8192]{2,1,0:T(2,128)(2,1)S(1)} all-gather(bf16[1,2,8192]{2,1,0:T(2,128)(2,1)S(1)} %reshape.965), channel_id=1, replica_groups=mesh['grp'=2,'beam'=16] {'beam'}, dimensions={0}, use_global_device_ids=true | all-gather | bytes 557056 | tf_op jit(solution)/shard_map/all_gather | solution.py:227
  519.0 5.0 fusion.36
  (461 shorter events, 207.0 us)
Async XLA Ops:
  0.0 104.8 %copy-start = (bf16[4,128,1024]{2,1,0:T(8,128)(2,1)S(1)}, bf16[4,128,1024]{2,1,0:T(8,128)(2,1)}, u32[]{:S(2)}) copy-start(bf16[4,128,1024]{2,1,0:T(8,128)(2,1)} %param.28) | copy-start | bytes 3145732
  39.1 27.4 %slice-start.6 = ((s8[8388608]{0:T(1024)(128)(4,1)}), s8[4194304]{0:T(1024)(128)(4,1)S(1)}, s32[]{:S(2)}) async-start(s8[8388608]{0:T(1024)(128)(4,1)} %bitcast.438), calls=%async_computation.15 | async-start | bytes 8388608
  39.1 27.3 %slice-start.7 = ((s8[8388608]{0:T(1024)(128)(4,1)}), s8[4194304]{0:T(1024)(128)(4,1)S(1)}, s32[]{:S(2)}) async-start(s8[8388608]{0:T(1024)(128)(4,1)} %bitcast.438), calls=%async_computation.16 | async-start | bytes 8388608
  45.1 23.5 %copy-start.41 = (bf16[32,640]{1,0:T(8,128)(2,1)}, bf16[32,640]{1,0:T(8,128)(2,1)S(1)}, u32[]{:S(2)}) copy-start(bf16[32,640]{1,0:T(8,128)(2,1)S(1)} %fusion.35) | copy-start | bytes 122884
  45.1 21.4 %copy-start.13 = (bf16[8192,128]{1,0:T(8,128)(2,1)S(1)}, bf16[8192,128]{1,0:T(8,128)(2,1)}, u32[]{:S(2)}) copy-start(bf16[8192,128]{1,0:T(8,128)(2,1)} %copy.303) | copy-start | bytes 6291460
  68.6 27.2 %copy-start.40 = (bf16[32,640]{1,0:T(8,128)(2,1)}, bf16[32,640]{1,0:T(8,128)(2,1)S(1)}, u32[]{:S(2)}) copy-start(bf16[32,640]{1,0:T(8,128)(2,1)S(1)} %fusion.33) | copy-start | bytes 122884
  96.5 80.4 %copy-start.70 = (pred[2,128]{1,0:T(4,128)(4,1)}, pred[2,128]{1,0:T(4,128)(4,1)S(1)}, u32[]{:S(2)}) copy-start(pred[2,128]{1,0:T(4,128)(4,1)S(1)} %broadcast_compare_fusion.6) | copy-start | bytes 772
  106.0 20.6 %slice-start.3 = ((bf16[32,640]{1,0:T(8,128)(2,1)}), bf16[32,512]{1,0:T(8,128)(2,1)S(1)}, s32[]{:S(2)}) async-start(bf16[32,640]{1,0:T(8,128)(2,1)} %copy-done.41), calls=%async_computation.12 | async-start | bytes 65536 | tf_op jit(solution)/shard_map/slice | solution.py:108
  289.4 14.9 %copy-start.36 = (f32[16,8,8,1,2]{0,4,2,1,3:T(2,128)S(1)}, f32[16,8,8,1,2]{0,4,2,1,3:T(2,128)}, u32[]{:S(2)}) copy-start(f32[16,8,8,1,2]{0,4,2,1,3:T(2,128)} %get-tuple-element.84) | copy-start | bytes 24580
  289.4 14.9 %copy-start.74 = (pred[16,2]{0,1:T(4,128)(4,1)S(1)}, pred[16,2]{0,1:T(4,128)(4,1)}, u32[]{:S(2)}) copy-start(pred[16,2]{0,1:T(4,128)(4,1)} %get-tuple-element.58) | copy-start | bytes 100
  326.0 9.9 %all-to-all-start = ((f32[16,1,128]{2,1,0:T(1,128)}), f32[16,1,128]{2,1,0:T(1,128)S(1)}, u32[]{:S(2)}, u32[]{:S(2)}) async-start(f32[16,1,128]{2,1,0:T(1,128)} %reshape.1020), calls=%async_computation | async-start | bytes 16384 | tf_op jit(solution)/shard_map/all_to_all | solution.py:199
  336.5 9.8 %all-to-all-start.8 = ((f32[16,1,128]{2,1,0:T(1,128)}), f32[16,1,128]{2,1,0:T(1,128)S(1)}, u32[]{:S(2)}, u32[]{:S(2)}) async-start(f32[16,1,128]{2,1,0:T(1,128)} %reshape.1014), calls=%async_computation.8 | async-start | bytes 16384 | tf_op jit(solution)/shard_map/all_to_all | solution.py:206
  346.3 10.2 %all-to-all-start.6 = ((f32[16,1,128]{2,1,0:T(1,128)}), f32[16,1,128]{2,1,0:T(1,128)S(1)}, u32[]{:S(2)}, u32[]{:S(2)}) async-start(f32[16,1,128]{2,1,0:T(1,128)} %reshape.1012), calls=%async_computation.6 | async-start | bytes 16384 | tf_op jit(solution)/shard_map/all_to_all | solution.py:199
  357.1 10.7 %all-to-all-start.5 = ((f32[16,1,128]{2,1,0:T(1,128)}), f32[16,1,128]{2,1,0:T(1,128)S(1)}, u32[]{:S(2)}, u32[]{:S(2)}) async-start(f32[16,1,128]{2,1,0:T(1,128)} %reshape.1018), calls=%async_computation.5 | async-start | bytes 16384 | tf_op jit(solution)/shard_map/all_to_all | solution.py:206
  361.4 14.7 %copy-start.51 = (f32[16,2,64]{2,1,0:T(2,128)S(1)}, f32[16,2,64]{2,1,0:T(2,128)}, u32[]{:S(2)}) copy-start(f32[16,2,64]{2,1,0:T(2,128)} %get-tuple-element.48) | copy-start | bytes 24580
  361.4 21.5 %copy-start.12 = (f32[2,16,8,8,128]{4,1,3,2,0:T(8,128)S(1)}, f32[2,16,8,8,128]{4,1,3,2,0:T(8,128)}, u32[]{:S(2)}) copy-start(f32[2,16,8,8,128]{4,1,3,2,0:T(8,128)} %get-tuple-element.80) | copy-start | bytes 3145732
  361.4 21.5 %copy-start.71 = (pred[2,128]{1,0:T(4,128)(4,1)S(1)}, pred[2,128]{1,0:T(4,128)(4,1)}, u32[]{:S(2)}) copy-start(pred[2,128]{1,0:T(4,128)(4,1)} %copy-done.70) | copy-start | bytes 772
  361.4 21.5 %copy-start.78 = (pred[2]{0:T(512)(128)(4,1)S(1)}, pred[2]{0:T(512)(128)(4,1)}, u32[]{:S(2)}) copy-start(pred[2]{0:T(512)(128)(4,1)} %iota_compare_fusion.1) | copy-start | bytes 10
  367.8 17.6 %copy-start.64 = (f32[16,1,128]{2,1,0:T(1,128)}, f32[16,1,128]{2,1,0:T(1,128)S(1)}, u32[]{:S(2)}) copy-start(f32[16,1,128]{2,1,0:T(1,128)S(1)} %all-to-all-done.5) | copy-start | bytes 24580
  367.8 10.9 %all-to-all-start.3 = ((f32[16,1,128]{2,1,0:T(1,128)}), f32[16,1,128]{2,1,0:T(1,128)S(1)}, u32[]{:S(2)}, u32[]{:S(2)}) async-start(f32[16,1,128]{2,1,0:T(1,128)} %reshape.1016), calls=%async_computation.3 | async-start | bytes 16384 | tf_op jit(solution)/shard_map/all_to_all | solution.py:199
  378.7 10.7 %all-to-all-start.2 = ((f32[16,1,128]{2,1,0:T(1,128)}), f32[16,1,128]{2,1,0:T(1,128)}, u32[]{:S(2)}, u32[]{:S(2)}) async-start(f32[16,1,128]{2,1,0:T(1,128)} %reshape.1022), calls=%async_computation.2 | async-start | bytes 16384 | tf_op jit(solution)/shard_map/all_to_all | solution.py:206
  389.4 20.3 %all-to-all-start.1 = ((bf16[16,2,8192]{2,1,0:T(2,128)(2,1)}), bf16[16,2,8192]{2,1,0:T(2,128)(2,1)}, u32[]{:S(2)}, u32[]{:S(2)}) async-start(bf16[16,2,8192]{2,1,0:T(2,128)(2,1)} %reshape.830), calls=%async_computation.1 | async-start | bytes 1048576 | tf_op jit(solution)/shard_map/all_to_all | solution.py:197
  409.7 18.6 %all-to-all-start.4 = ((bf16[16,2,8192]{2,1,0:T(2,128)(2,1)}), bf16[16,2,8192]{2,1,0:T(2,128)(2,1)S(1)}, u32[]{:S(2)}, u32[]{:S(2)}) async-start(bf16[16,2,8192]{2,1,0:T(2,128)(2,1)} %reshape.833), calls=%async_computation.4 | async-start | bytes 1048576 | tf_op jit(solution)/shard_map/all_to_all | solution.py:197
  428.3 18.8 %all-to-all-start.7 = ((bf16[16,2,8192]{2,1,0:T(2,128)(2,1)}), bf16[16,2,8192]{2,1,0:T(2,128)(2,1)S(1)}, u32[]{:S(2)}, u32[]{:S(2)}) async-start(bf16[16,2,8192]{2,1,0:T(2,128)(2,1)} %reshape.836), calls=%async_computation.7 | async-start | bytes 1048576 | tf_op jit(solution)/shard_map/all_to_all | solution.py:197
  (77 other events, 481.5 us)
where the time goes:
time: 536 us; the launch traced here: 525 us
  blocking collectives  250 us (47%)
  local copies, waits for them, and re-layouts  90 us (17%)
  matrix products  65 us (12%)
  other arithmetic  47.7 us (9%)
  starting transfers between devices  38 us (7%)
  waiting for transfers between devices  32.4 us (6%)
    all_gather x3, blocking collectives, local(): lax.all_gather(hidden[step], 'beam', axis=0, tiled=True).astype(jnp.float32)  71.2 us
    all_gather x3, blocking collectives, local(): lax.all_gather(attention, 'beam', axis=0, tiled=True)  60.5 us
    all_gather x3, blocking collectives, local(): lax.all_gather(kv_part, 'beam', axis=2, tiled=True)  59.7 us
    all_gather x3, blocking collectives, local(): lax.all_gather(q_part[:, None, :], 'beam', axis=2, tiled=True)  58.5 us
    unnamed x212, local copies, waits for them, and re-layouts  22 us
    all_to_all x3, waiting for transfers between devices, local(): lax.all_to_all(sending, 'beam', split_axis=0, concat_axis=0, tiled=True)  21.7 us
    dot_general x3, matrix products, local(): jnp.dot(lax.all_gather(attention, 'beam', axis=0, tiled=True), o_weight,...  14.8 us
    all_to_all x3, starting transfers between devices, local(): lax.all_to_all(sending, 'beam', split_axis=0, concat_axis=0, tiled=True)  14.3 us
  transfers between devices with their start and end apart: 9, of which 9 were waited for; matrix products, arithmetic and copies ran while one was open for 9% of the time, Pallas kernels for 0%

commit v1 on v0

--- a/solution.py
+++ b/solution.py
@@ -37,7 +37,7 @@
     )
 
 
-def local(
+def local_by_rows(
     hidden,
     norm_gain,
     q_weight,
@@ -232,6 +232,160 @@
     return jnp.stack(results, 0)
 
 
+def lineage_tables(parents, prefix_lens, tail_lens, rows_per_chip, devices):
+    all_rows = parents.shape[1]
+    row_ids = jnp.arange(all_rows, dtype=jnp.int32)
+    ancestors = row_ids
+    makers = []
+    anc_steps, pos_steps, maker_steps = [], [], []
+    base = prefix_lens[row_ids // BEAM_COUNT]
+    for step in range(STEPS):
+        hot = parents[step][:, None] == row_ids[None, :]
+        pick = lambda item: jnp.sum(jnp.where(hot, item[None, :], 0), axis=1)
+        ancestors = pick(ancestors)
+        makers = [pick(item) for item in makers] + [row_ids]
+        lens = jnp.sum(jnp.where(ancestors[:, None] == row_ids[None, :], tail_lens[None, :], 0), axis=1)
+        anc_steps.append(ancestors)
+        pos_steps.append(base + lens + step)
+        maker_steps.append(jnp.stack(makers + [jnp.full_like(row_ids, -1)] * (STEPS - 1 - step), 0))
+
+    def order(table):
+        lead = table.shape[1:-1]
+        table = table.reshape((STEPS,) + lead + (devices, rows_per_chip))
+        table = jnp.moveaxis(table, -2, 0)
+        table = jnp.moveaxis(table, 1, -2)
+        return jnp.moveaxis(table, 0, -3).reshape(lead + (STEPS * all_rows,))
+
+    return order(jnp.stack(anc_steps, 0)), order(jnp.stack(pos_steps, 0)), order(jnp.stack(maker_steps, 0))
+
+
+def local(
+    hidden,
+    norm_gain,
+    q_weight,
+    q_bias,
+    kv_weight,
+    kv_bias,
+    o_weight,
+    prefix_key_cache,
+    prefix_value_cache,
+    prefix_index,
+    prefix_lens,
+    tail_key_cache,
+    tail_value_cache,
+    tail_lens,
+    parents,
+):
+    devices = lax.axis_size("beam")
+    me = lax.axis_index("beam")
+    rpc = hidden.shape[1]
+    width = hidden.shape[2]
+    if QUERY_HEADS % devices or 2 * kv_weight.shape[2] != HEAD_DIM:
+        return local_by_rows(
+            hidden, norm_gain, q_weight, q_bias, kv_weight, kv_bias, o_weight, prefix_key_cache,
+            prefix_value_cache, prefix_index, prefix_lens, tail_key_cache, tail_value_cache, tail_lens, parents,
+        )
+    own = STEPS * rpc
+    rows = own * devices
+    prompts = prefix_index.shape[0]
+    ppr = rows // prompts
+    heads = QUERY_HEADS // devices
+    group = QUERY_HEADS // KEY_HEADS
+    q_cols = q_weight.shape[1]
+    kv_cols = kv_weight.shape[2]
+    slab = prefix_key_cache.shape[1]
+    tail = tail_key_cache.shape[1]
+    score_scale = 1.0 / math.sqrt(HEAD_DIM)
+    my_prompt = me * rpc // BEAM_COUNT
+    anc, pos, made = lineage_tables(parents, prefix_lens, tail_lens, rpc, devices)
+
+    x = hidden.astype(jnp.float32)
+    normed = (x * lax.rsqrt(jnp.mean(x * x, axis=-1, keepdims=True) + EPS) * norm_gain).astype(jnp.bfloat16)
+    normed = lax.all_gather(normed.reshape(own, width), "beam", axis=0, tiled=True)
+    q = (jnp.dot(normed, q_weight, preferred_element_type=jnp.float32) + q_bias).astype(jnp.bfloat16)
+    kv = jnp.dot(normed, kv_weight.reshape(width, 2 * kv_cols), preferred_element_type=jnp.float32)
+    kv = (kv + kv_bias.reshape(2 * kv_cols)).astype(jnp.bfloat16)
+    cosine, sine = rope_parts(pos, HEAD_DIM)
+    cosine2 = jnp.concatenate([cosine, cosine], 1)
+    sine2 = jnp.concatenate([-sine, sine], 1)
+
+    def rotate(v):
+        v = v.astype(jnp.float32)
+        return (v * cosine2 + jnp.roll(v, HEAD_DIM // 2, axis=-1) * sine2).astype(jnp.bfloat16)
+
+    pieces = [rotate(q[:, h * HEAD_DIM : (h + 1) * HEAD_DIM]) for h in range(heads)] + [kv]
+    full = lax.all_gather(jnp.stack(pieces, 0), "beam", axis=0)
+    query = full[:, :heads].reshape(KEY_HEADS, group, prompts, ppr, HEAD_DIM)
+    mine6 = lax.dynamic_slice_in_dim(full[:, heads], me * own, own, 1).reshape(devices, own, 2, kv_cols)
+    mine6 = jnp.transpose(mine6, (2, 1, 0, 3)).reshape(2, own, KEY_HEADS, HEAD_DIM)
+    my_cos = lax.dynamic_slice_in_dim(cosine2, me * own, own, 0)[:, None]
+    my_sin = lax.dynamic_slice_in_dim(sine2, me * own, own, 0)[:, None]
+    fk = mine6[0].astype(jnp.float32)
+    fk = (fk * my_cos + jnp.roll(fk, HEAD_DIM // 2, axis=-1) * my_sin).astype(jnp.bfloat16)
+    fv = mine6[1]
+
+    num, gmax, gsum = attend(
+        query, fk, fv, prefix_key_cache, prefix_value_cache, prefix_index, prefix_lens,
+        tail_key_cache, tail_value_cache, tail_lens, anc, made, me, my_prompt, rpc, score_scale,
+    )
+    parts = lax.all_to_all(num.reshape(devices, heads * rows, HEAD_DIM), "beam", 0, 0, tiled=True)
+    stats = jnp.stack([gmax.reshape(devices, heads, rows), gsum.reshape(devices, heads, rows)], 1)
+    stats = lax.all_to_all(stats, "beam", 0, 0, tiled=True)
+    maxima, sums = stats[:, 0], stats[:, 1]
+    factors = jnp.exp(maxima - maxima.max(0)[None])
+    denom = (factors * sums).sum(0)
+    parts = parts.reshape(devices, heads, rows, HEAD_DIM).astype(jnp.float32)
+    att = (factors[..., None] * parts).sum(0) / denom[..., None]
+    att = jnp.transpose(att.astype(jnp.bfloat16), (1, 0, 2)).reshape(rows, heads * HEAD_DIM)
+    att = lax.all_gather(att, "beam", axis=1, tiled=True)
+    out = jnp.dot(att, o_weight, preferred_element_type=jnp.float32).astype(jnp.bfloat16)
+    out = out.reshape(devices, STEPS, rpc, out.shape[1])
+    return jnp.transpose(out, (1, 0, 2, 3)).reshape(STEPS, devices * rpc, out.shape[3])
+
+
+def attend(
+    query, fk, fv, prefix_keys, prefix_values, prefix_index, prefix_lens,
+    tail_keys, tail_values, tail_lens, anc, made, me, my_prompt, rpc, score_scale,
+):
+    khs, group, prompts, ppr, hd = query.shape
+    slab = prefix_keys.shape[1]
+    tail = tail_keys.shape[1]
+    own = fk.shape[0]
+    rows = prompts * ppr
+    first = me * rpc
+    pk = jnp.take(prefix_keys, prefix_index, axis=0).reshape(prompts, slab, khs, hd)
+    pv = jnp.take(prefix_values, prefix_index, axis=0).reshape(prompts, slab, khs, hd)
+    s = jnp.einsum("kgpbd,pskd->kpgbs", query, pk, preferred_element_type=jnp.float32) * score_scale
+    ok = (me * slab + jnp.arange(slab, dtype=jnp.int32))[None, :] < prefix_lens[:, None]
+    ok = ok[None, :, None, None, :]
+    s = jnp.where(ok, s, NEG)
+    lq = lax.dynamic_index_in_dim(query, my_prompt, 2, keepdims=False).reshape(khs, group, ppr, hd)
+    lanc = lax.dynamic_slice_in_dim(anc, my_prompt * ppr, ppr, 0)
+    lmade = lax.dynamic_slice_in_dim(made, my_prompt * ppr, ppr, 1)
+    own_lens = lax.dynamic_slice_in_dim(tail_lens, first, rpc, 0)
+    slot = first + jnp.arange(rpc, dtype=jnp.int32)
+    t_ok = (lanc[:, None] == slot[None, :])[:, :, None] & (
+        jnp.arange(tail, dtype=jnp.int32)[None, None, :] < own_lens[None, :, None]
+    )
+    f_ok = lmade.T[:, :, None] == slot[None, None, :]
+    l_ok = jnp.concatenate([t_ok.reshape(ppr, rpc * tail), f_ok.reshape(ppr, own)], 1)[None, None]
+    lk = jnp.concatenate([tail_keys.reshape(rpc * tail, khs, hd), fk], 0)
+    lv = jnp.concatenate([tail_values.reshape(rpc * tail, khs, hd), fv], 0)
+    ls = jnp.einsum("kgbd,tkd->kgbt", lq, lk, preferred_element_type=jnp.float32) * score_scale
+    ls = jnp.where(l_ok, ls, NEG)
+    mine = (jnp.arange(prompts, dtype=jnp.int32) == my_prompt)[None, :, None, None]
+    gmax = jnp.maximum(s.max(-1), jnp.where(mine, ls.max(-1)[:, None], NEG))
+    lmax = lax.dynamic_index_in_dim(gmax, my_prompt, 1, keepdims=False)
+    w = jnp.where(ok, jnp.exp(s - gmax[..., None]), 0.0)
+    lw = jnp.where(l_ok, jnp.exp(ls - lmax[..., None]), 0.0)
+    gsum = w.sum(-1) + jnp.where(mine, lw.sum(-1)[:, None], 0.0)
+    num = jnp.einsum("kpgbs,pskd->kpgbd", w.astype(jnp.bfloat16), pv, preferred_element_type=jnp.float32)
+    lnum = jnp.einsum("kgbt,tkd->kgbd", lw.astype(jnp.bfloat16), lv, preferred_element_type=jnp.float32)
+    num = num + jnp.where(mine[..., None], lnum[:, None], 0.0)
+    num = jnp.swapaxes(num.astype(jnp.bfloat16), 1, 2).reshape(khs * group, rows, hd)
+    return num, jnp.swapaxes(gmax, 1, 2).reshape(khs * group, rows), jnp.swapaxes(gsum, 1, 2).reshape(khs * group, rows)
+
+
 def solution(mesh):
     return jax.shard_map(
         local,

time: 536 us -> 227 us (0.42); the launches traced: 525 us -> 227 us
  blocking collectives: 250 us -> 0 us
  waiting for transfers between devices: 32.4 us -> 138 us
  local copies, waits for them, and re-layouts: 90 us -> 26.8 us
  matrix products: 65 us -> 21.7 us
  other arithmetic: 47.7 us -> 17 us
  starting transfers between devices: 38 us -> 9.76 us
  between operations: 2.1 us -> 13.7 us
    all_gather x12 -> x0, blocking collectives: 250 us -> none  [the longest x3 71.2 us: local(): lax.all_gather(hidden[step], 'beam', axis=0, tiled=True).astype(jnp.float32)]
    all_gather x0 -> x3, waiting for transfers between devices: none -> 106 us  [the longest x1 43.5 us: local(): att = lax.all_gather(att, 'beam', axis=1, tiled=True)]
    dot_general x27 -> x7, matrix products: 65 us -> 21.7 us  [the longest x1 5.42 us: local(): jnp.dot(normed, q_weight, preferred_element_type=jnp.float32) + q_bias]
    all_to_all x9 -> x2, starting transfers between devices: 38 us -> 9.68 us  [the longest x1 5.96 us: local(): lax.all_to_all(num.reshape(devices, heads * rows, HEAD_DIM), 'beam', 0, 0...]
    unnamed x212 -> x48, local copies, waits for them, and re-layouts: 22 us -> 5.82 us
    reduce_max x9 -> x0, local copies, waits for them, and re-layouts: 11.9 us -> none  [the longest x6 7.95 us: local(): pre_max = pre_scores.max(-1)]
    reshape x18 -> x8, local copies, waits for them, and re-layouts: 13.4 us -> 4.92 us  [the longest x1 1.15 us: attend(): lv = jnp.concatenate([tail_values.reshape(rpc * tail, khs, hd), fv], 0)]
    add x12 -> x8, local copies, waits for them, and re-layouts: 8.5 us -> 1.29 us  [the longest x1 0.76 us: local(): kv = (kv + kv_bias.reshape(2 * kv_cols)).astype(jnp.bfloat16)]
  transfers between devices with their start and end apart: 9 -> 5, of which waited for: 9 -> 4; matrix products, arithmetic and copies ran while one was open for 9% -> 12% of each run, Pallas kernels for 0% -> 0%
where the time goes in v1:
time: 227 us
  waiting for transfers between devices  138 us (61%)
  local copies, waits for them, and re-layouts  26.8 us (12%)
  matrix products  21.7 us (10%)
  other arithmetic  17 us (7%)
  between operations  13.7 us (6%)
  starting transfers between devices  9.76 us (4%)
    all_gather x1, waiting for transfers between devices, local(): att = lax.all_gather(att, 'beam', axis=1, tiled=True)  43.5 us
    all_gather x1, waiting for transfers between devices, local(): lax.all_gather(normed.reshape(own, width), 'beam', axis=0, tiled=True)  34.8 us
    all_to_all x1, waiting for transfers between devices, local(): lax.all_to_all(num.reshape(devices, heads * rows, HEAD_DIM), 'beam', 0, 0...  31.7 us
    all_gather x1, waiting for transfers between devices, local(): full = lax.all_gather(jnp.stack(pieces, 0), 'beam', axis=0)  27.4 us
    all_to_all x1, starting transfers between devices, local(): lax.all_to_all(num.reshape(devices, heads * rows, HEAD_DIM), 'beam', 0, 0...  5.96 us
    unnamed x48, local copies, waits for them, and re-layouts  5.82 us
    dot_general x1, matrix products, local(): jnp.dot(normed, q_weight, preferred_element_type=jnp.float32) + q_bias  5.42 us
    dot_general x1, matrix products, local(): jnp.dot(att, o_weight, preferred_element_type=jnp.float32)  5.31 us
  transfers between devices with their start and end apart: 5, of which 4 were waited for; matrix products, arithmetic and copies ran while one was open for 12% of the time, Pallas kernels for 0%

profile of v1, /device:TPU:0, one launch (start us, length us, event | category | flops | bytes accessed | tf_op | source)
XLA Modules:
  0.0 226.6 jit_solution(15767145263596400857)
XLA Ops:
  6.5 1.3 fusion.31
  9.7 1.3 fusion.78
  13.9 1.3 add_add_fusion
  15.6 1.4 fusion.71
  19.0 34.8 %all-gather.10.cloned.1.call-done = bf16[16,6,8192]{2,1,0:T(8,128)(2,1)} async-done(((bf16[1,6,8192]{2,1,0:T(8,128)(2,1)}), bf16[16,6,8192]{2,1,0:T(8,128)(2,1)}) %all-gather.10.cloned.1.call-update) | async-done | bytes 1572880 | tf_op jit(solution)/shard_map/all_gather | solution.py:304
  53.9 2.7 %reshape.408 = bf16[96,8192]{1,0:T(8,128)(2,1)} reshape(bf16[16,6,8192]{2,1,0:T(8,128)(2,1)} %all-gather.10.cloned.1.call-done) | data formatting | bytes 3145728
  56.6 5.4 %fusion.18 = bf16[96,512]{1,0:T(8,128)(2,1)S(1)} fusion(bf16[96,8192]{1,0:T(8,128)(2,1)} %reshape.408, bf16[8192,512]{1,0:T(8,128)(2,1)} %param.20, f32[512]{0:T(512)S(1)} %copy-done.14), kind=kOutput, calls=%fused_computation.25 | convolution fusion | flops 805404672 | bytes 10061824 | tf_op jit(solution)/shard_map/dot_general | solution.py:305
  68.1 1.8 gather_fusion
  69.9 1.8 gather_fusion.1
  76.6 27.4 %all-gather.8.cloned.1.call-done = bf16[80,96,128]{2,1,0:T(8,128)(2,1)} async-done(((bf16[5,96,128]{2,1,0:T(8,128)(2,1)}), bf16[80,96,128]{2,1,0:T(8,128)(2,1)}) %all-gather.8.cloned.1.call-update) | async-done | bytes 1966096 | tf_op jit(solution)/shard_map/all_gather | solution.py:317
  105.1 2.7 %slice.117 = bf16[16,4,96,128]{3,2,1,0:T(8,128)(2,1)} slice(bf16[16,5,96,128]{3,2,1,0:T(8,128)(2,1)} %bitcast.156), slice={[0:16], [0:4], [0:96], [0:128]} | slice | bytes 3145728 | tf_op jit(solution)/shard_map/slice | solution.py:318
  108.4 2.6 %fusion.7 = (f32[8,2,8,48]{3,2,1,0:T(8,128)S(1)}, f32[8,2,8,48,128]{4,3,2,1,0:T(8,128)S(1)}) fusion(pred[2,128]{1,0:T(4,128)(4,1)S(1)} %broadcast_compare_fusion.2, bf16[2,128,8,128,1]{3,2,1,0,4:T(8,128)(2,1)S(1)} %copy-done.11, bf16[8,8,2,48,128]{4,3,2,1,0:T(8,128)(2,1)} %bitcast.157), kind=kOutput, calls=%fused_computation.14 | convolution fusion | flops 203679744 | bytes 5267712 | tf_op jit(solution)/shard_map/kgpbd,pskd->kpgbs/dot_general | solution.py:358
  111.2 1.5 fusion
  112.8 1.9 fusion.9
  114.7 2.6 %fusion.2 = f32[8,8,48]{2,1,0:T(8,128)S(1)} fusion(f32[8,8,48,518]{3,2,1,0:T(8,128)S(1)} %get-tuple-element.44, f32[8,8,48]{2,1,0:T(8,128)S(1)} %dynamic-slice_bitcast_fusion, pred[48,518]{1,0:T(8,128)(4,1)S(1)} %pad_add_fusion), kind=kLoop, calls=%fused_computation.6 | loop fusion | flops 7953408 | bytes 6414624 | tf_op jit(solution)/shard_map/reduce_sum | solution.py:381
  118.3 3.7 %all-to-all-start = ((f32[16,2,4,96]{3,2,1,0:T(4,128)}), f32[16,2,4,96]{3,2,1,0:T(4,128)S(1)}, u32[]{:S(2)}, u32[]{:S(2)}) async-start(f32[16,2,4,96]{3,2,1,0:T(4,128)} %copy.145), calls=%async_computation | async-start | bytes 131072 | tf_op jit(solution)/shard_map/all_to_all | solution.py:333
  122.1 4.6 %fusion.3 = f32[8,8,48,128]{3,2,1,0:T(8,128)S(1)} fusion(f32[8,8,48,518]{3,2,1,0:T(8,128)} %copy-done.2, f32[8,8,48]{2,1,0:T(8,128)S(1)} %dynamic-slice_bitcast_fusion, pred[48,518]{1,0:T(8,128)(4,1)S(1)} %pad_add_fusion, bf16[6,8,128]{2,0,1:T(8,128)(2,1)S(1)} %copy.149, bf16[512,8,128]{2,0,1:T(8,128)(2,1)S(1)} %copy-done.8), kind=kOutput, calls=%fused_computation.7 | convolution fusion | flops 417449984 | bytes 9036064 | tf_op jit(solution)/shard_map/kgbt,tkd->kgbd/dot_general | solution.py:383
  126.8 1.4 fusion.6
  128.2 1.3 copy.150
  129.4 6.0 %all-to-all-start.1 = ((bf16[16,384,128]{2,1,0:T(8,128)(2,1)}), bf16[16,384,128]{2,1,0:T(8,128)(2,1)}, u32[]{:S(2)}, u32[]{:S(2)}) async-start(bf16[16,384,128]{2,1,0:T(8,128)(2,1)} %bitcast.148), calls=%async_computation.1 | async-start | bytes 3145728 | tf_op jit(solution)/shard_map/all_to_all | solution.py:331
  135.7 31.7 %all-to-all-done.1 = bf16[16,384,128]{2,1,0:T(8,128)(2,1)} async-done(((bf16[16,384,128]{2,1,0:T(8,128)(2,1)}), bf16[16,384,128]{2,1,0:T(8,128)(2,1)}, u32[]{:S(2)}, u32[]{:S(2)}) %all-to-all-start.1) | async-done | bytes 1572896 | tf_op jit(solution)/shard_map/all_to_all | solution.py:331
  167.4 2.1 multiply_reduce_fusion
  170.4 43.5 %all-gather.6.cloned.1.call-done = bf16[96,8192]{1,0:T(8,128)(2,1)} async-done(((bf16[96,512]{1,0:T(8,128)(2,1)}), bf16[96,8192]{1,0:T(8,128)(2,1)}) %all-gather.6.cloned.1.call-update) | async-done | bytes 1572880 | tf_op jit(solution)/shard_map/all_gather | solution.py:340
  213.9 5.3 %convolution_convert_fusion = bf16[96,512]{1,0:T(8,128)(2,1)S(1)} fusion(bf16[96,8192]{1,0:T(8,128)(2,1)} %all-gather.6.cloned.1.call-done, bf16[8192,512]{1,0:T(8,128)(2,1)} %param.24), kind=kOutput, calls=%fused_computation.26 | convolution fusion | flops 805355520 | bytes 10059776 | tf_op jit(solution)/shard_map/dot_general | solution.py:341
  (158 shorter events, 22.6 us)
Async XLA Ops:
  6.5 56.2 %copy-start = (bf16[8192,2,64]{0,2,1:T(8,128)(2,1)S(1)}, bf16[8192,2,64]{0,2,1:T(8,128)(2,1)}, u32[]{:S(2)}) copy-start(bf16[8192,2,64]{0,2,1:T(8,128)(2,1)} %param.22) | copy-start | bytes 6291460
  6.5 50.0 %copy-start.14 = (f32[512]{0:T(512)S(1)}, f32[512]{0:T(512)}, u32[]{:S(2)}) copy-start(f32[512]{0:T(512)} %param.21) | copy-start | bytes 6148
  6.5 47.3 %all-gather.10.cloned.1.call-start = ((), (), s32[]{:S(2)}) async-start(), calls=%async_computation.4 | async-start | bytes 2228224 | tf_op jit(solution)/shard_map/all_gather | solution.py:304
  9.6 94.4 %all-gather.8.cloned.1.call-start = ((), (), s32[]{:S(2)}) async-start(), calls=%async_computation.3 | async-start | bytes 2088960 | tf_op jit(solution)/shard_map/all_gather | solution.py:317
  56.6 6.1 %copy-start.1 = (bf16[96,8192]{1,0:T(8,128)(2,1)S(1)}, bf16[96,8192]{1,0:T(8,128)(2,1)}, u32[]{:S(2)}) copy-start(bf16[96,8192]{1,0:T(8,128)(2,1)} %reshape.408) | copy-start | bytes 4718596
  62.0 3.5 %copy-start.16 = (s32[32]{0:T(128)S(1)}, s32[32]{0:T(128)}, u32[]{:S(2)}) copy-start(s32[32]{0:T(128)} %param.31) | copy-start | bytes 388
  62.0 4.1 %copy-start.13 = (s32[1,3,16,2]{2,3,1,0:T(2,128)S(1)}, s32[1,3,16,2]{2,3,1,0:T(2,128)}, u32[]{:S(2)}) copy-start(s32[1,3,16,2]{2,3,1,0:T(2,128)} %constant.87.clone.1) | copy-start | bytes 1156
  62.0 4.6 %copy-start.6 = (bf16[2,256,1024]{2,1,0:T(8,128)(2,1)S(1)}, bf16[2,256,1024]{2,1,0:T(8,128)(2,1)}, u32[]{:S(2)}) copy-start(bf16[2,256,1024]{2,1,0:T(8,128)(2,1)} %param.29) | copy-start | bytes 3145732
  63.6 0.7 copy-start.12
  63.6 4.5 %copy-start.17 = (s32[2]{0:T(128)S(1)}, s32[2]{0:T(128)}, u32[]{:S(2)}) copy-start(s32[2]{0:T(128)} %param.27) | copy-start | bytes 28
  71.8 1.2 copy-start.7
  72.0 2.9 %copy-start.15 = (s32[2]{0:T(128)S(1)}, s32[2]{0:T(128)}, u32[]{:S(2)}) copy-start(s32[2]{0:T(128)} %param.28) | copy-start | bytes 28
  75.7 32.6 %copy-start.11 = (bf16[2,128,8,128,1]{3,2,1,0,4:T(8,128)(2,1)S(1)}, bf16[2,128,8,128,1]{3,2,1,0,4:T(8,128)(2,1)}, u32[]{:S(2)}) copy-start(bf16[2,128,8,128,1]{3,2,1,0,4:T(8,128)(2,1)} %bitcast_bitcast_fusion.1) | copy-start | bytes 1572868
  108.3 2.8 %copy-start.5 = (bf16[16,4,96,128]{3,2,1,0:T(8,128)(2,1)S(1)}, bf16[16,4,96,128]{3,2,1,0:T(8,128)(2,1)}, u32[]{:S(2)}) copy-start(bf16[16,4,96,128]{3,2,1,0:T(8,128)(2,1)} %slice.117) | copy-start | bytes 4718596
  108.3 2.8 %copy-start.9 = (bf16[512,8,128]{2,0,1:T(8,128)(2,1)S(1)}, bf16[512,8,128]{2,0,1:T(8,128)(2,1)}, u32[]{:S(2)}) copy-start(bf16[512,8,128]{2,0,1:T(8,128)(2,1)} %copy.142) | copy-start | bytes 3145732
  111.0 1.7 copy-start.3
  112.7 4.5 %copy-start.2 = (f32[8,8,48,518]{3,2,1,0:T(8,128)}, f32[8,8,48,518]{3,2,1,0:T(8,128)S(1)}, u32[]{:S(2)}) copy-start(f32[8,8,48,518]{3,2,1,0:T(8,128)S(1)} %get-tuple-element.44) | copy-start | bytes 19095556
  114.7 7.5 %copy-start.8 = (bf16[512,8,128]{2,0,1:T(8,128)(2,1)S(1)}, bf16[512,8,128]{2,0,1:T(8,128)(2,1)}, u32[]{:S(2)}) copy-start(bf16[512,8,128]{2,0,1:T(8,128)(2,1)} %copy.148) | copy-start | bytes 3145732
  118.3 11.1 %all-to-all-start = ((f32[16,2,4,96]{3,2,1,0:T(4,128)}), f32[16,2,4,96]{3,2,1,0:T(4,128)S(1)}, u32[]{:S(2)}, u32[]{:S(2)}) async-start(f32[16,2,4,96]{3,2,1,0:T(4,128)} %copy.145), calls=%async_computation | async-start | bytes 131072 | tf_op jit(solution)/shard_map/all_to_all | solution.py:333
  122.1 4.6 %copy-start.4 = (f32[8,2,8,48,128]{4,3,2,1,0:T(8,128)S(1)}, f32[8,2,8,48,128]{4,3,2,1,0:T(8,128)}, u32[]{:S(2)}) copy-start(f32[8,2,8,48,128]{4,3,2,1,0:T(8,128)} %copy-done.3) | copy-start | bytes 9437188
  122.1 4.6 %copy-start.10 = (bf16[2,128,8,128,1]{3,2,1,0,4:T(8,128)(2,1)S(1)}, bf16[2,128,8,128,1]{3,2,1,0,4:T(8,128)(2,1)}, u32[]{:S(2)}) copy-start(bf16[2,128,8,128,1]{3,2,1,0,4:T(8,128)(2,1)} %bitcast_bitcast_fusion) | copy-start | bytes 1572868
  129.4 38.0 %all-to-all-start.1 = ((bf16[16,384,128]{2,1,0:T(8,128)(2,1)}), bf16[16,384,128]{2,1,0:T(8,128)(2,1)}, u32[]{:S(2)}, u32[]{:S(2)}) async-start(bf16[16,384,128]{2,1,0:T(8,128)(2,1)} %bitcast.148), calls=%async_computation.1 | async-start | bytes 3145728 | tf_op jit(solution)/shard_map/all_to_all | solution.py:331
  135.4 78.5 %all-gather.6.cloned.1.call-start = ((), (), s32[]{:S(2)}) async-start(), calls=%async_computation.2 | async-start | bytes 1671168 | tf_op jit(solution)/shard_map/all_gather | solution.py:340
Sparse Core Ops, SparseCore 0:
  9.7 44.0 all-gather.9
  64.4 39.6 all-gather.7
  170.5 43.3 all-gather.5

commit v2 on v1

--- a/solution.py
+++ b/solution.py
@@ -4,6 +4,8 @@
 import jax.numpy as jnp
 import numpy as np
 from jax import lax
+from jax.experimental import pallas as pl
+from jax.experimental.pallas import tpu as pltpu
 from jax.sharding import PartitionSpec as P
 
 QUERY_HEADS = 64
@@ -232,6 +234,243 @@
     return jnp.stack(results, 0)
 
 
+MESH = pl.DeviceIdType.MESH
+
+
+def place():
+    me = lax.axis_index("beam")
+    return me, me // 4, me // 2 % 2, me % 2
+
+
+def at(z, y, c):
+    return (z * 2 + y) * 2 + c
+
+
+def partners(z):
+    return [z + 1 - 2 * (z % 2), (z + 2) % 4, 3 - z]
+
+
+def greet(z, y, c):
+    barrier = pltpu.get_barrier_semaphore()
+    others = [at(w, y, c) for w in partners(z)] + [at(z, 1 - y, c), at(z, y, 1 - c)]
+    for other in others:
+        pl.semaphore_signal(barrier, inc=1, device_id={"beam": other}, device_id_type=MESH)
+    pl.semaphore_wait(barrier, len(others))
+
+
+class Gather:
+    def __init__(self, x_ref, o_ref, send, recv):
+        self.x_ref, self.o_ref, self.send, self.recv = x_ref, o_ref, send, recv
+        self.me, self.z, self.y, self.c = place()
+        self.sent = []
+
+    def push(self, shard, target, src):
+        copy = pltpu.make_async_remote_copy(
+            src_ref=src,
+            dst_ref=self.o_ref.at[shard],
+            send_sem=self.send.at[len(self.sent)],
+            recv_sem=self.recv.at[shard],
+            device_id={"beam": target},
+            device_id_type=MESH,
+        )
+        copy.start()
+        self.sent.append(copy)
+
+    def arrive(self, shard):
+        pltpu.make_async_remote_copy(
+            src_ref=self.o_ref.at[shard],
+            dst_ref=self.o_ref.at[shard],
+            send_sem=self.send.at[0],
+            recv_sem=self.recv.at[shard],
+            device_id={"beam": at(self.z, self.y, 1 - self.c)},
+            device_id_type=MESH,
+        ).wait_recv()
+
+    def run(self, use):
+        z, y, c = self.z, self.y, self.c
+        over, core = at(z, 1 - y, c), at(z, y, 1 - c)
+        zs = partners(z)
+        self.push(self.me, over, self.x_ref)
+        for w in zs[::-1]:
+            self.push(self.me, at(w, y, c), self.x_ref)
+        self.push(self.me, core, self.x_ref)
+        use(self.me)
+        for k, w in enumerate([z] + zs):
+            if k:
+                shard = at(w, y, c)
+                self.arrive(shard)
+                self.push(shard, over, self.o_ref.at[shard])
+                self.push(shard, core, self.o_ref.at[shard])
+                use(shard)
+        for w in [z] + zs:
+            shard = at(w, 1 - y, c)
+            self.arrive(shard)
+            self.push(shard, core, self.o_ref.at[shard])
+            use(shard)
+        for w in [z] + zs:
+            for v in (y, 1 - y):
+                shard = at(w, v, 1 - c)
+                self.arrive(shard)
+                use(shard)
+        for copy in self.sent:
+            copy.wait_send()
+
+
+def gather_kernel(x_ref, o_ref, send, recv):
+    me, z, y, c = place()
+    greet(z, y, c)
+    o_ref[me] = x_ref[...]
+    Gather(x_ref, o_ref, send, recv).run(lambda shard: None)
+
+
+def gather(x, devices, tag):
+    vmem = pl.BlockSpec(memory_space=pltpu.VMEM)
+    return pl.pallas_call(
+        gather_kernel,
+        out_shape=jax.ShapeDtypeStruct((devices,) + x.shape, x.dtype),
+        in_specs=[vmem],
+        out_specs=vmem,
+        scratch_shapes=[pltpu.SemaphoreType.DMA((15,)), pltpu.SemaphoreType.DMA((16,))],
+        compiler_params=pltpu.CompilerParams(
+            collective_id=tag, has_side_effects=True, vmem_limit_bytes=32 * 2**20
+        ),
+    )(x)
+
+
+def merge_kernel(
+    heads, rows, num_ref, st_ref, ow_ref, out_ref,
+    in1, st1, acc1, sacc1, in2, st2, acc2, sacc2, in3, st3, att, full, weight,
+    send, recv, gsend, grecv, wsem,
+):
+    me, z, y, c = place()
+    fetch = pltpu.make_async_copy(ow_ref, weight, wsem)
+    fetch.start()
+    greet(z, y, c)
+    over, core = at(z, 1 - y, c), at(z, y, 1 - c)
+    order = partners(z)[::-1] + [z]
+    started = []
+
+    def ship(src, ssrc, dst, sdst, target):
+        slot = len(started)
+        for copy_src, copy_dst, lane in ((src, dst, 0), (ssrc, sdst, 1)):
+            pltpu.make_async_remote_copy(
+                src_ref=copy_src, dst_ref=copy_dst, send_sem=send.at[slot, lane], recv_sem=recv.at[slot, lane],
+                device_id={"beam": target}, device_id_type=MESH,
+            ).start()
+        started.append((src, ssrc, dst, sdst, target))
+
+    def handle(slot, lane):
+        src, ssrc, dst, sdst, target = started[slot]
+        return pltpu.make_async_remote_copy(
+            src_ref=(src, ssrc)[lane], dst_ref=(dst, sdst)[lane], send_sem=send.at[slot, lane],
+            recv_sem=recv.at[slot, lane], device_id={"beam": target}, device_id_type=MESH,
+        )
+
+    def landed(slot):
+        handle(slot, 0).wait_recv()
+        handle(slot, 1).wait_recv()
+
+    def weigh(stats):
+        top = stats[0][:heads]
+        for item in stats[1:]:
+            top = jnp.maximum(top, item[:heads])
+        scale = [jnp.exp(item[:heads] - top) for item in stats]
+        total = scale[0] * stats[0][heads:]
+        for e, item in zip(scale[1:], stats[1:]):
+            total = total + e * item[heads:]
+        return top, scale, total
+
+    def flip(top_half, low_half):
+        return jnp.transpose(jnp.concatenate([top_half, low_half], 0))
+
+    def merge(a, sa, b, sb, dst, sdst):
+        top, scale, total = weigh([sa[...], sb[...]])
+        sdst[...] = jnp.concatenate([top, total], 0)
+        e = flip(scale[0], scale[1])
+        for h in range(heads):
+            part = pl.ds(h * rows, rows)
+            dst[part, :] = (
+                a[part, :].astype(jnp.float32) * e[:rows, h : h + 1]
+                + b[part, :].astype(jnp.float32) * e[:rows, heads + h : heads + h + 1]
+            ).astype(jnp.bfloat16)
+
+    for v, base in ((1 - y, 0), (y, 4)):
+        for k, w in enumerate(order):
+            chunk = at(w, v, 1 - c)
+            ship(num_ref.at[chunk], st_ref.at[chunk], in1.at[base + k], st1.at[base + k], core)
+    for k, w in enumerate(order):
+        chunk = at(w, 1 - y, c)
+        landed(k)
+        merge(num_ref.at[chunk], st_ref.at[chunk], in1.at[k], st1.at[k], acc1.at[k], sacc1.at[k])
+        ship(acc1.at[k], sacc1.at[k], in2.at[k], st2.at[k], over)
+    for k, w in enumerate(order):
+        chunk = at(w, y, c)
+        landed(4 + k)
+        merge(num_ref.at[chunk], st_ref.at[chunk], in1.at[4 + k], st1.at[4 + k], acc1.at[4 + k], sacc1.at[4 + k])
+    for k, w in enumerate(order):
+        landed(8 + k)
+        merge(acc1.at[4 + k], sacc1.at[4 + k], in2.at[k], st2.at[k], acc2.at[k], sacc2.at[k])
+        if k < 3:
+            ship(acc2.at[k], sacc2.at[k], in3.at[k], st3.at[k], at(w, y, c))
+    for k in range(3):
+        landed(12 + k)
+    stats = [sacc2[3]] + [st3[k] for k in range(3)]
+    top, scale, total = weigh(stats)
+    e01, e23 = flip(scale[0], scale[1]), flip(scale[2], scale[3])
+    below = flip(total, total)
+    for h in range(heads):
+        part = pl.ds(h * rows, rows)
+        value = acc2[3, part, :].astype(jnp.float32) * e01[:rows, h : h + 1]
+        for k, table, lane in ((0, e01, heads + h), (1, e23, h), (2, e23, heads + h)):
+            value = value + in3[k, part, :].astype(jnp.float32) * table[:rows, lane : lane + 1]
+        att[:, h * HEAD_DIM : (h + 1) * HEAD_DIM] = (value / below[:rows, h : h + 1]).astype(jnp.bfloat16)
+    full[me] = att[...]
+    fetch.wait()
+    depth = heads * HEAD_DIM
+    total = [None]
+
+    def use(shard):
+        term = jnp.dot(
+            full[shard], weight[pl.ds(shard * depth, depth), :], preferred_element_type=jnp.float32
+        )
+        total[0] = term if total[0] is None else total[0] + term
+
+    Gather(att, full, gsend, grecv).run(use)
+    out_ref[...] = total[0].astype(jnp.bfloat16)
+    for slot in range(len(started)):
+        handle(slot, 0).wait_send()
+        handle(slot, 1).wait_send()
+
+
+def merge_and_project(num, stats, o_weight, heads, rows, tag):
+    devices = num.shape[0]
+    vmem = pl.BlockSpec(memory_space=pltpu.VMEM)
+    chunk = num.shape[1:]
+    depth, cols = o_weight.shape
+    bf = lambda k: pltpu.VMEM((k,) + chunk, jnp.bfloat16)
+    fl = lambda k: pltpu.VMEM((k,) + stats.shape[1:], jnp.float32)
+    return pl.pallas_call(
+        lambda *refs: merge_kernel(heads, rows, *refs),
+        out_shape=jax.ShapeDtypeStruct((rows, cols), jnp.bfloat16),
+        in_specs=[vmem, vmem, pl.BlockSpec(memory_space=pl.ANY)],
+        out_specs=vmem,
+        scratch_shapes=[
+            bf(8), fl(8), bf(8), fl(8), bf(4), fl(4), bf(4), fl(4), bf(3), fl(3),
+            pltpu.VMEM((rows, heads * HEAD_DIM), jnp.bfloat16),
+            pltpu.VMEM((devices, rows, heads * HEAD_DIM), jnp.bfloat16),
+            pltpu.VMEM((depth, cols), jnp.bfloat16),
+            pltpu.SemaphoreType.DMA((15, 2)),
+            pltpu.SemaphoreType.DMA((15, 2)),
+            pltpu.SemaphoreType.DMA((15,)),
+            pltpu.SemaphoreType.DMA((16,)),
+            pltpu.SemaphoreType.DMA,
+        ],
+        compiler_params=pltpu.CompilerParams(
+            collective_id=tag, has_side_effects=True, vmem_limit_bytes=40 * 2**20
+        ),
+    )(num, stats, o_weight)
+
+
 def lineage_tables(parents, prefix_lens, tail_lens, rows_per_chip, devices):
     all_rows = parents.shape[1]
     row_ids = jnp.arange(all_rows, dtype=jnp.int32)
@@ -280,7 +519,7 @@
     me = lax.axis_index("beam")
     rpc = hidden.shape[1]
     width = hidden.shape[2]
-    if QUERY_HEADS % devices or 2 * kv_weight.shape[2] != HEAD_DIM:
+    if devices != 16 or 2 * kv_weight.shape[2] != HEAD_DIM or STEPS * rpc > 8:
         return local_by_rows(
             hidden, norm_gain, q_weight, q_bias, kv_weight, kv_bias, o_weight, prefix_key_cache,
             prefix_value_cache, prefix_index, prefix_lens, tail_key_cache, tail_value_cache, tail_lens, parents,
@@ -301,10 +540,13 @@
 
     x = hidden.astype(jnp.float32)
     normed = (x * lax.rsqrt(jnp.mean(x * x, axis=-1, keepdims=True) + EPS) * norm_gain).astype(jnp.bfloat16)
-    normed = lax.all_gather(normed.reshape(own, width), "beam", axis=0, tiled=True)
+    normed = jnp.pad(normed.reshape(own, width), ((0, 8 - own), (0, 0)))
+    normed = gather(normed, devices, 0).reshape(devices * 8, width)
+    real = lambda v: v.reshape(devices, 8, v.shape[1])[:, :own].reshape(rows, v.shape[1])
     q = (jnp.dot(normed, q_weight, preferred_element_type=jnp.float32) + q_bias).astype(jnp.bfloat16)
     kv = jnp.dot(normed, kv_weight.reshape(width, 2 * kv_cols), preferred_element_type=jnp.float32)
     kv = (kv + kv_bias.reshape(2 * kv_cols)).astype(jnp.bfloat16)
+    q, kv = real(q), real(kv)
     cosine, sine = rope_parts(pos, HEAD_DIM)
     cosine2 = jnp.concatenate([cosine, cosine], 1)
     sine2 = jnp.concatenate([-sine, sine], 1)
@@ -314,7 +556,7 @@
         return (v * cosine2 + jnp.roll(v, HEAD_DIM // 2, axis=-1) * sine2).astype(jnp.bfloat16)
 
     pieces = [rotate(q[:, h * HEAD_DIM : (h + 1) * HEAD_DIM]) for h in range(heads)] + [kv]
-    full = lax.all_gather(jnp.stack(pieces, 0), "beam", axis=0)
+    full = gather(jnp.stack(pieces, 0), devices, 1)
     query = full[:, :heads].reshape(KEY_HEADS, group, prompts, ppr, HEAD_DIM)
     mine6 = lax.dynamic_slice_in_dim(full[:, heads], me * own, own, 1).reshape(devices, own, 2, kv_cols)
     mine6 = jnp.transpose(mine6, (2, 1, 0, 3)).reshape(2, own, KEY_HEADS, HEAD_DIM)
@@ -328,17 +570,9 @@
         query, fk, fv, prefix_key_cache, prefix_value_cache, prefix_index, prefix_lens,
         tail_key_cache, tail_value_cache, tail_lens, anc, made, me, my_prompt, rpc, score_scale,
     )
-    parts = lax.all_to_all(num.reshape(devices, heads * rows, HEAD_DIM), "beam", 0, 0, tiled=True)
-    stats = jnp.stack([gmax.reshape(devices, heads, rows), gsum.reshape(devices, heads, rows)], 1)
-    stats = lax.all_to_all(stats, "beam", 0, 0, tiled=True)
-    maxima, sums = stats[:, 0], stats[:, 1]
-    factors = jnp.exp(maxima - maxima.max(0)[None])
-    denom = (factors * sums).sum(0)
-    parts = parts.reshape(devices, heads, rows, HEAD_DIM).astype(jnp.float32)
-    att = (factors[..., None] * parts).sum(0) / denom[..., None]
-    att = jnp.transpose(att.astype(jnp.bfloat16), (1, 0, 2)).reshape(rows, heads * HEAD_DIM)
-    att = lax.all_gather(att, "beam", axis=1, tiled=True)
-    out = jnp.dot(att, o_weight, preferred_element_type=jnp.float32).astype(jnp.bfloat16)
+    stats = jnp.concatenate([gmax.reshape(devices, heads, rows), gsum.reshape(devices, heads, rows)], 1)
+    stats = jnp.pad(stats, ((0, 0), (0, 0), (0, 128 - rows)))
+    out = merge_and_project(num.reshape(devices, heads * rows, HEAD_DIM), stats, o_weight, heads, rows, 2)
     out = out.reshape(devices, STEPS, rpc, out.shape[1])
     return jnp.transpose(out, (1, 0, 2, 3)).reshape(STEPS, devices * rpc, out.shape[3])
 

time: 227 us -> 143 us (0.63)
  waiting for transfers between devices: 138 us -> 0 us
  Pallas kernels: 0 us -> 82.2 us
  between operations: 13.7 us -> 0.57 us
  starting transfers between devices: 9.76 us -> 0 us
  local copies, waits for them, and re-layouts: 26.8 us -> 22.6 us
  matrix products: 21.7 us -> 19.3 us
    all_gather x3 -> x0, waiting for transfers between devices: 106 us -> none  [the longest x1 43.5 us: local(): att = lax.all_gather(att, 'beam', axis=1, tiled=True)]
    pallas_call x0 -> x3, Pallas kernels: none -> 82.2 us  [the longest x2 47.6 us: gather(): pl.pallas_call(gather_kernel, out_shape=jax.ShapeDtypeStruct((devices,) +...]
    all_to_all x2 -> x0, waiting for transfers between devices: 31.7 us -> none  [the longest x1 31.7 us: local(): lax.all_to_all(num.reshape(devices, heads * rows, HEAD_DIM), 'beam', 0, 0...]
    all_to_all x2 -> x0, starting transfers between devices: 9.68 us -> none  [the longest x1 5.96 us: local(): lax.all_to_all(num.reshape(devices, heads * rows, HEAD_DIM), 'beam', 0, 0...]
    dot_general x1 -> x0, matrix products: 5.31 us -> none  [local(): jnp.dot(att, o_weight, preferred_element_type=jnp.float32)]
    dot_general x1, matrix products: 1.52 us -> 4.52 us  [attend(): jnp.einsum('kgbd,tkd->kgbt', lq, lk, preferred_element_type=jnp.float32)]
    unnamed x48 -> x41, local copies, waits for them, and re-layouts: 5.82 us -> 6.22 us
  transfers between devices with their start and end apart: 5 -> 0, of which waited for: 4 -> 0; matrix products, arithmetic and copies ran while one was open for 12% -> 0% of each run, Pallas kernels for 0% -> 0%
where the time goes in v2:
time: 143 us; the launch traced here: 142 us
  Pallas kernels  82.2 us (57%)
  local copies, waits for them, and re-layouts  22.6 us (16%)
  matrix products  19.3 us (13%)
  other arithmetic  17.2 us (12%)
    pallas_call x2, Pallas kernels, gather(): pl.pallas_call(gather_kernel, out_shape=jax.ShapeDtypeStruct((devices,) +...  47.6 us
    pallas_call x1, Pallas kernels, merge_and_project(): pl.pallas_call(lambda *refs: merge_kernel(heads, rows, *refs), out_shape=...  34.6 us
    reduce_sum x2, other arithmetic, attend(): gsum = w.sum(-1) + jnp.where(mine, lw.sum(-1)[:, None], 0.0)  6.51 us
    unnamed x41, local copies, waits for them, and re-layouts  6.22 us
    dot_general x1, matrix products, local(): jnp.dot(normed, q_weight, preferred_element_type=jnp.float32) + q_bias  5.4 us
    dot_general x1, matrix products, attend(): jnp.einsum('kgbt,tkd->kgbd', lw.astype(jnp.bfloat16), lv, preferred_eleme...  4.63 us
    dot_general x1, matrix products, attend(): jnp.einsum('kgbd,tkd->kgbt', lq, lk, preferred_element_type=jnp.float32)  4.52 us

profile of v2, /device:TPU:0, one launch (start us, length us, event | category | flops | bytes accessed | tf_op | source)
XLA Modules:
  0.0 141.9 jit_solution(13296157285787591059)
XLA Ops:
  3.0 1.3 fusion.91
  4.3 1.3 add_add_fusion
  6.0 1.4 fusion.85
  8.7 1.1 fusion.49
  9.8 1.1 fusion.51
  11.0 26.1 %shard_map.154 = bf16[16,8,8192]{2,1,0:T(8,128)(2,1)S(1)} custom-call(bf16[8,8192]{1,0:T(8,128)(2,1)S(1)} %pad.9.x_ref), custom_call_target="tpu_custom_call" | custom-call | tf_op jit(solution)/shard_map/pallas_call | solution.py:328
  37.2 5.4 %fusion.28 = bf16[16,8,512]{2,1,0:T(8,128)(2,1)S(1)} fusion(bf16[8192,512]{1,0:T(8,128)(2,1)} %param.20, bf16[16,8,8192]{2,1,0:T(8,128)(2,1)S(1)} %shard_map.154, f32[512]{0:T(512)S(1)} %copy-done.9), kind=kOutput, calls=%fused_computation.29 | convolution fusion | flops 1073872896 | bytes 10618880 | tf_op jit(solution)/shard_map/dot_general | solution.py:546
  43.4 2.3 %fusion.37 = bf16[16,8,128]{2,1,0:T(8,128)(2,1)S(1)} fusion(bf16[8192,128]{0,1:T(8,128)(2,1)S(1)} %bitcast.133, bf16[16,8,8192]{2,1,0:T(8,128)(2,1)} %copy-done.1, f32[128]{0:T(128)S(1)} %add.208), kind=kOutput, calls=%fused_computation.32 | convolution fusion | flops 268468224 | bytes 4227584 | tf_op jit(solution)/shard_map/dot_general | solution.py:547
  45.8 21.5 %shard_map.155 = bf16[16,5,96,128]{3,2,1,0:T(8,128)(2,1)S(1)} custom-call(bf16[5,96,128]{2,1,0:T(8,128)(2,1)S(1)} %constant_dynamic-update-slice_fusion.x_ref), custom_call_target="tpu_custom_call" | custom-call | tf_op jit(solution)/shard_map/pallas_call | solution.py:328
  67.3 1.3 copy-done.2
  70.9 2.8 %slice.92 = bf16[16,4,96,128]{3,2,1,0:T(8,128)(2,1)} slice(bf16[16,5,96,128]{3,2,1,0:T(8,128)(2,1)} %copy-done.2), slice={[0:16], [0:4], [0:96], [0:128]} | slice | bytes 3145728 | tf_op jit(solution)/shard_map/slice | solution.py:560
  76.7 1.0 copy-done.5
  77.6 4.5 %fusion = (f32[8,8,48]{2,1,0:T(8,128)S(1)}, f32[8,8,48,518]{3,2,1,0:T(8,128)}) fusion(pred[48,518]{1,0:T(8,128)(4,1)S(1)} %pad_add_fusion, bf16[6,8,128]{2,0,1:T(8,128)(2,1)S(1)} %fusion.62, bf16[512,8,128]{2,0,1:T(8,128)(2,1)S(1)} %copy.119, bf16[8,8,2,48,128]{4,3,2,1,0:T(8,128)(2,1)S(1)} %bitcast.143, s32[]{:T(128)S(6)} %select_n.129), kind=kOutput, calls=%fused_computation.4 | convolution fusion | flops 414264320 | bytes 8259588 | tf_op jit(solution)/shard_map/kgbd,tkd->kgbt/dot_general | solution.py:608
  82.2 1.8 %gather_fusion = bf16[2,128,1024]{2,1,0:T(8,128)(2,1)S(1)} fusion(bf16[4,128,1024]{2,1,0:T(8,128)(2,1)} %param.25, s32[1024]{0:T(1024)S(1)} %pad_clamp_fusion), kind=kCustom, calls=%fused_computation.clone | custom fusion | bytes 1048584 | tf_op jit(solution)/shard_map/jit(_take)/gather | solution.py:590
  84.1 2.6 %gather_fusion.1 = bf16[2,128,1024]{2,1,0:T(8,128)(2,1)} fusion(bf16[4,128,1024]{2,1,0:T(8,128)(2,1)} %param.26, s32[1024]{0:T(1024)S(1)} %pad_clamp_fusion), kind=kCustom, calls=%fused_computation.1.clone | custom fusion | bytes 1048584 | tf_op jit(solution)/shard_map/jit(_take)/gather | solution.py:591
  86.7 1.3 broadcast_select_fusion
  88.2 1.1 fusion.7
  89.4 1.6 %copy-done.3 = f32[8,2,8,48,128]{4,3,2,1,0:T(8,128)} copy-done((f32[8,2,8,48,128]{4,3,2,1,0:T(8,128)}, f32[8,2,8,48,128]{4,3,2,1,0:T(8,128)S(1)}, u32[]{:S(2)}) %copy-start.3) | copy-done | bytes 3145752
  91.0 1.9 %fusion.8 = f32[8,2,8,48]{3,2,1,0:T(8,128)S(1)} fusion(f32[8,2,8,48,128]{4,3,2,1,0:T(8,128)S(1)} %get-tuple-element.42, f32[8,2,8,48]{3,2,1,0:T(8,128)S(1)} %select_maximum_fusion.1, pred[2,128]{1,0:T(4,128)(4,1)S(1)} %broadcast_compare_fusion.2), kind=kLoop, calls=%fused_computation.14 | loop fusion | flops 3926016 | bytes 3195136 | tf_op jit(solution)/shard_map/reduce_sum | solution.py:615
  92.9 4.7 %fusion.1 = f32[8,8,48]{2,1,0:T(8,128)S(1)} fusion(f32[8,8,48,518]{3,2,1,0:T(8,128)} %get-tuple-element.44, f32[8,8,48]{2,1,0:T(8,128)S(1)} %dynamic-slice_bitcast_fusion, pred[48,518]{1,0:T(8,128)(4,1)S(1)} %pad_add_fusion), kind=kLoop, calls=%fused_computation.5 | loop fusion | flops 7953408 | bytes 6414624 | tf_op jit(solution)/shard_map/reduce_sum | solution.py:615
  98.3 1.5 %copy.140 = bf16[64,8,8,128]{3,2,1,0:T(8,128)(2,1)S(1)} copy(bf16[64,8,8,128]{3,1,2,0:T(8,128)(2,1)} %bitcast.146) | data formatting | bytes 2097152
  100.0 4.6 %fusion.3 = f32[8,8,48,128]{3,2,1,0:T(8,128)S(1)} fusion(f32[8,8,48,518]{3,2,1,0:T(8,128)} %get-tuple-element.44, f32[8,8,48]{2,1,0:T(8,128)S(1)} %dynamic-slice_bitcast_fusion, pred[48,518]{1,0:T(8,128)(4,1)S(1)} %pad_add_fusion, bf16[6,8,128]{2,0,1:T(8,128)(2,1)S(1)} %copy.122, bf16[512,8,128]{2,0,1:T(8,128)(2,1)S(1)} %copy.121), kind=kOutput, calls=%fused_computation.7 | convolution fusion | flops 417449984 | bytes 9036064 | tf_op jit(solution)/shard_map/kgbt,tkd->kgbd/dot_general | solution.py:617
  104.7 1.4 fusion.6
  106.5 34.6 %shard_map.156 = bf16[96,512]{1,0:T(8,128)(2,1)S(1)} custom-call(bf16[16,384,128]{2,1,0:T(8,128)(2,1)S(1)} %bitcast.136, f32[16,8,128]{2,1,0:T(8,128)S(1)} %select_maximum_fusion.refs_1_, bf16[8192,512]{1,0:T(8,128)(2,1)S(1)} %bitcast.135), custom_call_target="tpu_custom_call" | custom-call | tf_op jit(solution)/shard_map/pallas_call | solution.py:452
  (138 shorter events, 13.2 us)
Async XLA Ops:
  0.0 43.4 %copy-start = (bf16[8192,2,64]{0,2,1:T(8,128)(2,1)S(1)}, bf16[8192,2,64]{0,2,1:T(8,128)(2,1)}, u32[]{:S(2)}) copy-start(bf16[8192,2,64]{0,2,1:T(8,128)(2,1)} %param.22) | copy-start | bytes 6291460
  0.0 37.2 %copy-start.9 = (f32[512]{0:T(512)S(1)}, f32[512]{0:T(512)}, u32[]{:S(2)}) copy-start(f32[512]{0:T(512)} %param.21) | copy-start | bytes 6148
  37.2 5.4 %copy-start.1 = (bf16[16,8,8192]{2,1,0:T(8,128)(2,1)}, bf16[16,8,8192]{2,1,0:T(8,128)(2,1)S(1)}, u32[]{:S(2)}) copy-start(bf16[16,8,8192]{2,1,0:T(8,128)(2,1)S(1)} %shard_map.154) | copy-start | bytes 6291460
  37.2 6.2 %copy-start.12 = (f32[2,64]{1,0:T(2,128)S(1)}, f32[2,64]{1,0:T(2,128)}, u32[]{:S(2)}) copy-start(f32[2,64]{1,0:T(2,128)} %param.23) | copy-start | bytes 1540
  45.8 29.0 %copy-start.11 = (s32[32]{0:T(128)S(1)}, s32[32]{0:T(128)}, u32[]{:S(2)}) copy-start(s32[32]{0:T(128)} %param.31) | copy-start | bytes 388
  67.3 1.3 copy-start.2
  68.5 7.0 %copy-start.8 = (s32[1,3,16,2]{2,3,1,0:T(2,128)S(1)}, s32[1,3,16,2]{2,3,1,0:T(2,128)}, u32[]{:S(2)}) copy-start(s32[1,3,16,2]{2,3,1,0:T(2,128)} %constant.90.clone.1) | copy-start | bytes 1156
  68.5 7.7 %copy-start.7 = (bf16[2,256,1024]{2,1,0:T(8,128)(2,1)S(1)}, bf16[2,256,1024]{2,1,0:T(8,128)(2,1)}, u32[]{:S(2)}) copy-start(bf16[2,256,1024]{2,1,0:T(8,128)(2,1)} %param.29) | copy-start | bytes 3145732
  76.2 1.4 copy-start.5
  77.6 4.5 %copy-start.10 = (s32[2]{0:T(128)S(1)}, s32[2]{0:T(128)}, u32[]{:S(2)}) copy-start(s32[2]{0:T(128)} %param.28) | copy-start | bytes 28
  77.6 4.6 %copy-start.13 = (s32[2]{0:T(128)S(1)}, s32[2]{0:T(128)}, u32[]{:S(2)}) copy-start(s32[2]{0:T(128)} %param.27) | copy-start | bytes 28
  86.7 1.6 %copy-start.6 = (bf16[16,4,96,128]{3,2,1,0:T(8,128)(2,1)S(1)}, bf16[16,4,96,128]{3,2,1,0:T(8,128)(2,1)}, u32[]{:S(2)}) copy-start(bf16[16,4,96,128]{3,2,1,0:T(8,128)(2,1)} %slice.92) | copy-start | bytes 4718596
  89.3 1.7 %copy-start.3 = (f32[8,2,8,48,128]{4,3,2,1,0:T(8,128)}, f32[8,2,8,48,128]{4,3,2,1,0:T(8,128)S(1)}, u32[]{:S(2)}) copy-start(f32[8,2,8,48,128]{4,3,2,1,0:T(8,128)S(1)} %get-tuple-element.42) | copy-start | bytes 9437188
  99.8 6.5 %slice-start = ((s8[8388608]{0:T(1024)(128)(4,1)}), s8[4194304]{0:T(1024)(128)(4,1)S(1)}, s32[]{:S(2)}) async-start(s8[8388608]{0:T(1024)(128)(4,1)} %bitcast.134), calls=%async_computation | async-start | bytes 8388608
  99.9 4.8 %copy-start.4 = (f32[8,2,8,48,128]{4,3,2,1,0:T(8,128)S(1)}, f32[8,2,8,48,128]{4,3,2,1,0:T(8,128)}, u32[]{:S(2)}) copy-start(f32[8,2,8,48,128]{4,3,2,1,0:T(8,128)} %copy-done.3) | copy-start | bytes 9437188
  99.9 6.5 %slice-start.1 = ((s8[8388608]{0:T(1024)(128)(4,1)}), s8[4194304]{0:T(1024)(128)(4,1)S(1)}, s32[]{:S(2)}) async-start(s8[8388608]{0:T(1024)(128)(4,1)} %bitcast.134), calls=%async_computation.1 | async-start | bytes 8388608

commit v3 on v2

--- a/solution.py
+++ b/solution.py
@@ -471,6 +471,163 @@
     )(num, stats, o_weight)
 
 
+def attend_kernel(
+    own, scale, x_ref, pk_ref, pv_ref, tk_ref, tv_ref, pok_ref, lok_ref, cs_ref, sn_ref,
+    num_ref, st_ref, full, column, send, recv,
+):
+    me, z, y, c = place()
+    greet(z, y, c)
+    full[me] = x_ref[...]
+    column[...] = jnp.zeros_like(column)
+    over, core = at(z, 1 - y, c), at(z, y, 1 - c)
+    heads = x_ref.shape[0] - 1
+    rows = x_ref.shape[1]
+    ppr = rows // 2
+    tail = tk_ref.shape[0]
+    my_prompt = me // 8
+    group = 2 * heads
+
+    def push(slot, shard, target, src):
+        pltpu.make_async_remote_copy(
+            src_ref=src, dst_ref=full.at[shard], send_sem=send.at[slot], recv_sem=recv.at[shard],
+            device_id={"beam": target}, device_id_type=MESH,
+        ).start()
+
+    def arrive(shard):
+        pltpu.make_async_remote_copy(
+            src_ref=full.at[shard], dst_ref=full.at[shard], send_sem=send.at[0], recv_sem=recv.at[shard],
+            device_id={"beam": core}, device_id_type=MESH,
+        ).wait_recv()
+
+    zs = partners(z)
+    push(0, me, over, x_ref)
+    for k in (2, 1, 0):
+        push(1 + k, me, at(zs[k], y, c), x_ref)
+    push(4, me, core, x_ref)
+    for k, w in enumerate(zs):
+        shard = at(w, y, c)
+        arrive(shard)
+        push(5 + 2 * k, shard, over, full.at[shard])
+        push(6 + 2 * k, shard, core, full.at[shard])
+
+    lane = lax.broadcasted_iota(jnp.int32, (16, HEAD_DIM), 1)
+    pick_row = lax.broadcasted_iota(jnp.int32, (16, rows), 0)
+    pick_col = lax.broadcasted_iota(jnp.int32, (16, rows), 1)
+    hot = jnp.where((pick_col == me * own + pick_row) & (pick_row < own), 1.0, 0.0).astype(jnp.bfloat16)
+    wide = lax.broadcasted_iota(jnp.int32, (ppr, 128), 1)
+    contract = (((1,), (1,)), ((), ()))
+
+    def queries(k, prompt):
+        start = pl.multiple_of(prompt * ppr, 16)
+        return jnp.concatenate(
+            [full[2 * k + g // heads, g % heads, pl.ds(start, ppr), :] for g in range(group)], 0
+        )
+
+    def write(k, prompt, num, top, total):
+        start = pl.multiple_of(prompt * ppr, 16)
+        num = num.astype(jnp.bfloat16)
+        table = jnp.zeros((ppr, 128), jnp.float32)
+        for g in range(group):
+            part = slice(g * ppr, (g + 1) * ppr)
+            place_at = pl.multiple_of(g % heads * rows + prompt * ppr, 16)
+            num_ref[2 * k + g // heads, pl.ds(place_at, ppr), :] = num[part]
+            base = g // heads * 2 * heads + g % heads
+            table = jnp.where(wide == base, top[part], table)
+            table = jnp.where(wide == base + heads, total[part], table)
+        column[pl.ds(start, ppr), :] = table
+
+    def one(i, carry):
+        w = (z // 2 + i % 4 // 2) % 2 * 2 + (z + i) % 2
+        v = (y + i // 4) % 2
+
+        @pl.when(i < 4)
+        def _():
+            shard = at(w, 1 - y, c)
+            arrive(shard)
+            push(11 + i, shard, core, full.at[shard])
+
+        arrive(at(w, v, 1 - c))
+        k = w * 2 + v
+        cols = pl.ds(pl.multiple_of(k * HEAD_DIM, HEAD_DIM), HEAD_DIM)
+        lo = jnp.dot(hot, full[2 * k, heads], preferred_element_type=jnp.float32)
+        hi = jnp.dot(hot, full[2 * k + 1, heads], preferred_element_type=jnp.float32)
+        key = jnp.where(lane < HEAD_DIM // 2, lo, pltpu.roll(hi, HEAD_DIM // 2, 1))
+        value = jnp.where(lane < HEAD_DIM // 2, pltpu.roll(lo, HEAD_DIM // 2, 1), hi)
+        key = key * cs_ref[...] + pltpu.roll(key, HEAD_DIM // 2, 1) * sn_ref[...]
+        blank = jnp.zeros((128 - 16, HEAD_DIM), jnp.bfloat16)
+        key = jnp.concatenate([key.astype(jnp.bfloat16), blank], 0)
+        value = jnp.concatenate([value.astype(jnp.bfloat16), blank], 0)
+
+        def prefix(prompt, q):
+            keys = pk_ref[prompt, :, cols]
+            s = lax.dot_general(q, keys, contract, preferred_element_type=jnp.float32) * scale
+            ok = pok_ref[prompt][:1] > 0.0
+            return jnp.where(ok, s, NEG), ok
+
+        q = queries(k, 1 - my_prompt)
+        s, ok = prefix(1 - my_prompt, q)
+        top = jnp.max(s, axis=1, keepdims=True)
+        e = jnp.where(ok, jnp.exp(s - top), 0.0)
+        num = jnp.dot(e.astype(jnp.bfloat16), pv_ref[1 - my_prompt, :, cols], preferred_element_type=jnp.float32)
+        write(k, 1 - my_prompt, num, top, jnp.sum(e, axis=1, keepdims=True))
+
+        q = queries(k, my_prompt)
+        s, ok = prefix(my_prompt, q)
+        ls = jnp.concatenate(
+            [
+                lax.dot_general(q, tk_ref[:, cols], contract, preferred_element_type=jnp.float32),
+                lax.dot_general(q, key, contract, preferred_element_type=jnp.float32),
+            ],
+            1,
+        )
+        lok = jnp.concatenate([lok_ref[...]] * group, 0) > 0.0
+        ls = jnp.where(lok, ls * scale, NEG)
+        top = jnp.maximum(jnp.max(s, axis=1, keepdims=True), jnp.max(ls, axis=1, keepdims=True))
+        e = jnp.where(ok, jnp.exp(s - top), 0.0)
+        le = jnp.where(lok, jnp.exp(ls - top), 0.0)
+        total = jnp.sum(e, axis=1, keepdims=True) + jnp.sum(le, axis=1, keepdims=True)
+        le = le.astype(jnp.bfloat16)
+        num = jnp.dot(e.astype(jnp.bfloat16), pv_ref[my_prompt, :, cols], preferred_element_type=jnp.float32)
+        num = num + jnp.dot(le[:, :tail], tv_ref[:, cols], preferred_element_type=jnp.float32)
+        num = num + jnp.dot(le[:, tail:], value, preferred_element_type=jnp.float32)
+        write(k, my_prompt, num, top, total)
+
+        flat = jnp.transpose(column[...])
+        st_ref[2 * k] = flat[: 2 * heads]
+        st_ref[2 * k + 1] = flat[2 * heads : 4 * heads]
+        return carry
+
+    lax.fori_loop(0, 8, one, 0)
+    for slot in range(15):
+        pltpu.make_async_remote_copy(
+            src_ref=x_ref, dst_ref=full.at[0], send_sem=send.at[slot], recv_sem=recv.at[0],
+            device_id={"beam": core}, device_id_type=MESH,
+        ).wait_send()
+
+
+def gather_and_attend(pieces, pk, pv, tk, tv, pok, lok, cs, sn, own, scale, devices, tag):
+    vmem = pl.BlockSpec(memory_space=pltpu.VMEM)
+    heads, rows = pieces.shape[0] - 1, pieces.shape[1]
+    return pl.pallas_call(
+        lambda *refs: attend_kernel(own, scale, *refs),
+        out_shape=[
+            jax.ShapeDtypeStruct((devices, heads * rows, HEAD_DIM), jnp.bfloat16),
+            jax.ShapeDtypeStruct((devices, 2 * heads, 128), jnp.float32),
+        ],
+        in_specs=[vmem] * 9,
+        out_specs=[vmem, vmem],
+        scratch_shapes=[
+            pltpu.VMEM((devices,) + pieces.shape, jnp.bfloat16),
+            pltpu.VMEM((128, 128), jnp.float32),
+            pltpu.SemaphoreType.DMA((15,)),
+            pltpu.SemaphoreType.DMA((16,)),
+        ],
+        compiler_params=pltpu.CompilerParams(
+            collective_id=tag, has_side_effects=True, vmem_limit_bytes=40 * 2**20
+        ),
+    )(pieces, pk, pv, tk, tv, pok, lok, cs, sn)
+
+
 def lineage_tables(parents, prefix_lens, tail_lens, rows_per_chip, devices):
     all_rows = parents.shape[1]
     row_ids = jnp.arange(all_rows, dtype=jnp.int32)
@@ -519,7 +676,7 @@
     me = lax.axis_index("beam")
     rpc = hidden.shape[1]
     width = hidden.shape[2]
-    if devices != 16 or 2 * kv_weight.shape[2] != HEAD_DIM or STEPS * rpc > 8:
+    if devices != 16 or 2 * kv_weight.shape[2] != HEAD_DIM or STEPS * rpc > 8 or prefix_index.shape[0] != 2:
         return local_by_rows(
             hidden, norm_gain, q_weight, q_bias, kv_weight, kv_bias, o_weight, prefix_key_cache,
             prefix_value_cache, prefix_index, prefix_lens, tail_key_cache, tail_value_cache, tail_lens, parents,
@@ -556,68 +713,32 @@
         return (v * cosine2 + jnp.roll(v, HEAD_DIM // 2, axis=-1) * sine2).astype(jnp.bfloat16)
 
     pieces = [rotate(q[:, h * HEAD_DIM : (h + 1) * HEAD_DIM]) for h in range(heads)] + [kv]
-    full = gather(jnp.stack(pieces, 0), devices, 1)
-    query = full[:, :heads].reshape(KEY_HEADS, group, prompts, ppr, HEAD_DIM)
-    mine6 = lax.dynamic_slice_in_dim(full[:, heads], me * own, own, 1).reshape(devices, own, 2, kv_cols)
-    mine6 = jnp.transpose(mine6, (2, 1, 0, 3)).reshape(2, own, KEY_HEADS, HEAD_DIM)
-    my_cos = lax.dynamic_slice_in_dim(cosine2, me * own, own, 0)[:, None]
-    my_sin = lax.dynamic_slice_in_dim(sine2, me * own, own, 0)[:, None]
-    fk = mine6[0].astype(jnp.float32)
-    fk = (fk * my_cos + jnp.roll(fk, HEAD_DIM // 2, axis=-1) * my_sin).astype(jnp.bfloat16)
-    fv = mine6[1]
-
-    num, gmax, gsum = attend(
-        query, fk, fv, prefix_key_cache, prefix_value_cache, prefix_index, prefix_lens,
-        tail_key_cache, tail_value_cache, tail_lens, anc, made, me, my_prompt, rpc, score_scale,
-    )
-    stats = jnp.concatenate([gmax.reshape(devices, heads, rows), gsum.reshape(devices, heads, rows)], 1)
-    stats = jnp.pad(stats, ((0, 0), (0, 0), (0, 128 - rows)))
-    out = merge_and_project(num.reshape(devices, heads * rows, HEAD_DIM), stats, o_weight, heads, rows, 2)
-    out = out.reshape(devices, STEPS, rpc, out.shape[1])
-    return jnp.transpose(out, (1, 0, 2, 3)).reshape(STEPS, devices * rpc, out.shape[3])
-
-
-def attend(
-    query, fk, fv, prefix_keys, prefix_values, prefix_index, prefix_lens,
-    tail_keys, tail_values, tail_lens, anc, made, me, my_prompt, rpc, score_scale,
-):
-    khs, group, prompts, ppr, hd = query.shape
-    slab = prefix_keys.shape[1]
-    tail = tail_keys.shape[1]
-    own = fk.shape[0]
-    rows = prompts * ppr
     first = me * rpc
-    pk = jnp.take(prefix_keys, prefix_index, axis=0).reshape(prompts, slab, khs, hd)
-    pv = jnp.take(prefix_values, prefix_index, axis=0).reshape(prompts, slab, khs, hd)
-    s = jnp.einsum("kgpbd,pskd->kpgbs", query, pk, preferred_element_type=jnp.float32) * score_scale
-    ok = (me * slab + jnp.arange(slab, dtype=jnp.int32))[None, :] < prefix_lens[:, None]
-    ok = ok[None, :, None, None, :]
-    s = jnp.where(ok, s, NEG)
-    lq = lax.dynamic_index_in_dim(query, my_prompt, 2, keepdims=False).reshape(khs, group, ppr, hd)
+    slot = first + jnp.arange(rpc, dtype=jnp.int32)
     lanc = lax.dynamic_slice_in_dim(anc, my_prompt * ppr, ppr, 0)
     lmade = lax.dynamic_slice_in_dim(made, my_prompt * ppr, ppr, 1)
     own_lens = lax.dynamic_slice_in_dim(tail_lens, first, rpc, 0)
-    slot = first + jnp.arange(rpc, dtype=jnp.int32)
     t_ok = (lanc[:, None] == slot[None, :])[:, :, None] & (
         jnp.arange(tail, dtype=jnp.int32)[None, None, :] < own_lens[None, :, None]
     )
     f_ok = lmade.T[:, :, None] == slot[None, None, :]
-    l_ok = jnp.concatenate([t_ok.reshape(ppr, rpc * tail), f_ok.reshape(ppr, own)], 1)[None, None]
-    lk = jnp.concatenate([tail_keys.reshape(rpc * tail, khs, hd), fk], 0)
-    lv = jnp.concatenate([tail_values.reshape(rpc * tail, khs, hd), fv], 0)
-    ls = jnp.einsum("kgbd,tkd->kgbt", lq, lk, preferred_element_type=jnp.float32) * score_scale
-    ls = jnp.where(l_ok, ls, NEG)
-    mine = (jnp.arange(prompts, dtype=jnp.int32) == my_prompt)[None, :, None, None]
-    gmax = jnp.maximum(s.max(-1), jnp.where(mine, ls.max(-1)[:, None], NEG))
-    lmax = lax.dynamic_index_in_dim(gmax, my_prompt, 1, keepdims=False)
-    w = jnp.where(ok, jnp.exp(s - gmax[..., None]), 0.0)
-    lw = jnp.where(l_ok, jnp.exp(ls - lmax[..., None]), 0.0)
-    gsum = w.sum(-1) + jnp.where(mine, lw.sum(-1)[:, None], 0.0)
-    num = jnp.einsum("kpgbs,pskd->kpgbd", w.astype(jnp.bfloat16), pv, preferred_element_type=jnp.float32)
-    lnum = jnp.einsum("kgbt,tkd->kgbd", lw.astype(jnp.bfloat16), lv, preferred_element_type=jnp.float32)
-    num = num + jnp.where(mine[..., None], lnum[:, None], 0.0)
-    num = jnp.swapaxes(num.astype(jnp.bfloat16), 1, 2).reshape(khs * group, rows, hd)
-    return num, jnp.swapaxes(gmax, 1, 2).reshape(khs * group, rows), jnp.swapaxes(gsum, 1, 2).reshape(khs * group, rows)
+    lok = jnp.concatenate([t_ok.reshape(ppr, rpc * tail), f_ok.reshape(ppr, own)], 1).astype(jnp.float32)
+    lok = jnp.pad(lok, ((0, 0), (0, 128 - own)))
+    pok = (me * slab + jnp.arange(slab, dtype=jnp.int32))[None, :] < prefix_lens[:, None]
+    pok = jnp.broadcast_to(pok.astype(jnp.float32)[:, None], (prompts, 8, slab))
+    my_cos = jnp.pad(lax.dynamic_slice_in_dim(cosine2, me * own, own, 0), ((0, 16 - own), (0, 0)))
+    my_sin = jnp.pad(lax.dynamic_slice_in_dim(sine2, me * own, own, 0), ((0, 16 - own), (0, 0)))
+    num, stats = gather_and_attend(
+        jnp.stack(pieces, 0),
+        jnp.take(prefix_key_cache, prefix_index, axis=0, mode="clip"),
+        jnp.take(prefix_value_cache, prefix_index, axis=0, mode="clip"),
+        tail_key_cache.reshape(rpc * tail, -1),
+        tail_value_cache.reshape(rpc * tail, -1),
+        pok, lok, my_cos, my_sin, own, score_scale, devices, 1,
+    )
+    out = merge_and_project(num, stats, o_weight, heads, rows, 2)
+    out = out.reshape(devices, STEPS, rpc, out.shape[1])
+    return jnp.transpose(out, (1, 0, 2, 3)).reshape(STEPS, devices * rpc, out.shape[3])
 
 
 def solution(mesh):

time: 143 us -> 121 us (0.85)
  matrix products: 19.3 us -> 7.75 us
  other arithmetic: 17.2 us -> 8.88 us
  local copies, waits for them, and re-layouts: 22.6 us -> 15.8 us
  Pallas kernels: 82.2 us -> 88.1 us
    pallas_call x0 -> x1, Pallas kernels: none -> 25.7 us  [gather_and_attend(): pl.pallas_call(lambda *refs: attend_kernel(own, scale, *refs), out_shape=...]
    pallas_call x2 -> x1, Pallas kernels: 47.6 us -> 26.1 us  [gather(): pl.pallas_call(gather_kernel, out_shape=jax.ShapeDtypeStruct((devices,) +...]
    dot_general x4 -> x0, matrix products: 11.6 us -> none  [the longest x1 4.63 us: attend(): jnp.einsum('kgbt,tkd->kgbd', lw.astype(jnp.bfloat16), lv, preferred_eleme...]
    reduce_sum x2 -> x0, other arithmetic: 6.51 us -> none  [attend(): gsum = w.sum(-1) + jnp.where(mine, lw.sum(-1)[:, None], 0.0)]
    slice x4 -> x0, local copies, waits for them, and re-layouts: 3.83 us -> none  [the longest x1 2.79 us: local(): query = full[:, :heads].reshape(KEY_HEADS, group, prompts, ppr, HEAD_DIM)]
    pallas_call x1, Pallas kernels: 34.6 us -> 36.2 us  [merge_and_project(): pl.pallas_call(lambda *refs: merge_kernel(heads, rows, *refs), out_shape=...]
    unnamed x41 -> x25, local copies, waits for them, and re-layouts: 6.22 us -> 5.88 us
where the time goes in v3:
time: 121 us
  Pallas kernels  88.1 us (73%)
  local copies, waits for them, and re-layouts  15.8 us (13%)
  other arithmetic  8.88 us (7%)
  matrix products  7.75 us (6%)
    pallas_call x1, Pallas kernels, merge_and_project(): pl.pallas_call(lambda *refs: merge_kernel(heads, rows, *refs), out_shape=...  36.2 us
    pallas_call x1, Pallas kernels, gather(): pl.pallas_call(gather_kernel, out_shape=jax.ShapeDtypeStruct((devices,) +...  26.1 us
    pallas_call x1, Pallas kernels, gather_and_attend(): pl.pallas_call(lambda *refs: attend_kernel(own, scale, *refs), out_shape=...  25.7 us
    unnamed x25, local copies, waits for them, and re-layouts  5.88 us
    dot_general x1, matrix products, local(): jnp.dot(normed, q_weight, preferred_element_type=jnp.float32) + q_bias  5.4 us
    add x2, other arithmetic, lineage_tables(): pos_steps.append(base + lens + step)  2.7 us

profile of v3, /device:TPU:0, one launch (start us, length us, event | category | flops | bytes accessed | tf_op | source)
XLA Modules:
  0.0 120.8 jit_solution(18152280794214407426)
XLA Ops:
  0.0 0.9 slice_bitcast_fusion
  0.9 0.2 select_reduce_fusion.8
  1.1 0.2 select_reduce_fusion.2
  1.2 0.9 select_reduce_fusion.1
  2.2 1.3 %fusion.51 = (s32[1]{0:T(128)}, s32[1]{0:T(128)}) fusion(s32[2]{0:T(128)} %param.26), kind=kLoop, calls=%fused_computation.102 | loop fusion | bytes 16 | tf_op jit(solution)/shard_map/gather | solution.py:637
  3.5 1.3 %add_add_fusion.1 = (s32[32]{0:T(128)S(1)}, s32[32]{0:T(128)S(1)}) fusion(s32[32]{0:T(128)S(1)} %get-tuple-element.12, s32[]{:T(128)} %bitcast.3, s32[]{:T(128)} %bitcast.2, s32[32]{0:T(128)S(1)} %get-tuple-element.13), kind=kLoop, calls=%fused_computation.94 | loop fusion | flops 512 | bytes 520 | tf_op jit(solution)/shard_map/add | solution.py:645
  5.2 0.8 select_reduce_fusion.3
  6.0 1.4 %add_add_fusion = s32[32]{0:T(128)S(1)} fusion(s32[32]{0:T(128)S(1)} %select_reduce_fusion.3, s32[]{:T(128)} %bitcast.3, s32[]{:T(128)} %bitcast.2), kind=kLoop, calls=%fused_computation.92 | loop fusion | flops 480 | bytes 264 | tf_op jit(solution)/shard_map/add | solution.py:645
  7.7 0.1 convert_element_type.70
  7.8 0.9 fusion.41
  8.7 1.1 fusion.22
  9.8 1.1 fusion.24
  11.0 26.1 %shard_map.154 = bf16[16,8,8192]{2,1,0:T(8,128)(2,1)S(1)} custom-call(bf16[8,8192]{1,0:T(8,128)(2,1)S(1)} %pad.18.x_ref), custom_call_target="tpu_custom_call" | custom-call | tf_op jit(solution)/shard_map/pallas_call | solution.py:328
  37.2 5.4 %fusion.10 = bf16[16,8,512]{2,1,0:T(8,128)(2,1)S(1)} fusion(bf16[8192,512]{1,0:T(8,128)(2,1)} %param.18, bf16[16,8,8192]{2,1,0:T(8,128)(2,1)S(1)} %shard_map.154, f32[512]{0:T(512)S(1)} %copy-done.7), kind=kOutput, calls=%fused_computation.8 | convolution fusion | flops 1073872896 | bytes 10618880 | tf_op jit(solution)/shard_map/dot_general | solution.py:703
  43.4 2.3 %fusion.19 = bf16[16,8,128]{2,1,0:T(8,128)(2,1)S(1)} fusion(bf16[8192,128]{0,1:T(8,128)(2,1)S(1)} %bitcast.79, bf16[16,8,8192]{2,1,0:T(8,128)(2,1)} %copy-done.1, f32[128]{0:T(128)S(1)} %add.187), kind=kOutput, calls=%fused_computation.11 | convolution fusion | flops 268468224 | bytes 4227584 | tf_op jit(solution)/shard_map/dot_general | solution.py:704
  46.5 0.1 reshape.314
  48.6 1.8 %gather_fusion = bf16[2,128,1024]{2,1,0:T(8,128)(2,1)S(1)} fusion(bf16[4,128,1024]{2,1,0:T(8,128)(2,1)} %param.23, s32[1024]{0:T(1024)S(1)} %pad_clamp_fusion), kind=kCustom, calls=%fused_computation | custom fusion | bytes 1048584 | tf_op jit(solution)/shard_map/jit(_take)/gather | solution.py:733
  50.4 1.8 %gather_fusion.1 = bf16[2,128,1024]{2,1,0:T(8,128)(2,1)S(1)} fusion(bf16[4,128,1024]{2,1,0:T(8,128)(2,1)} %param.24, s32[1024]{0:T(1024)S(1)} %pad_clamp_fusion), kind=kCustom, calls=%fused_computation.1 | custom fusion | bytes 1048584 | tf_op jit(solution)/shard_map/jit(_take)/gather | solution.py:734
  52.2 1.2 %copy-done.3 = bf16[2,256,1024]{2,1,0:T(8,128)(2,1)S(1)} copy-done((bf16[2,256,1024]{2,1,0:T(8,128)(2,1)S(1)}, bf16[2,256,1024]{2,1,0:T(8,128)(2,1)}, u32[]{:S(2)}) %copy-start.3) | copy-done | bytes 1048600
  53.5 1.2 %copy-done.4 = bf16[2,256,1024]{2,1,0:T(8,128)(2,1)S(1)} copy-done((bf16[2,256,1024]{2,1,0:T(8,128)(2,1)S(1)}, bf16[2,256,1024]{2,1,0:T(8,128)(2,1)}, u32[]{:S(2)}) %copy-start.4) | copy-done | bytes 1048600
  54.7 25.7 %shard_map.155 = (bf16[16,384,128]{2,1,0:T(8,128)(2,1)S(1)}, f32[16,8,128]{2,1,0:T(8,128)S(1)}) custom-call(bf16[5,96,128]{2,1,0:T(8,128)(2,1)S(1)} %constant_dynamic-update-slice_fusion.refs_0_, bf16[2,128,1024]{2,1,0:T(8,128)(2,1)S(1)} %gather_fusion, bf16[2,128,1024]{2,1,0:T(8,128)(2,1)S(1)} %gather_fusion.1, bf16[512,1024]{1,0:T(8,128)(2,1)S(1)} %bitcast.80, ...), custom_call_target="tpu_custom_call" | custom-call | tf_op jit(solution)/shard_map/pallas_call | solution.py:611
  80.4 3.4 %copy-done.2 = bf16[8192,512]{1,0:T(8,128)(2,1)S(1)} copy-done((bf16[8192,512]{1,0:T(8,128)(2,1)S(1)}, bf16[8192,512]{1,0:T(8,128)(2,1)}, u32[]{:S(2)}) %copy-start.2) | copy-done | bytes 8388632
  83.8 36.2 %shard_map.156 = bf16[96,512]{1,0:T(8,128)(2,1)S(1)} custom-call(bf16[16,384,128]{2,1,0:T(8,128)(2,1)S(1)} %get-tuple-element.7.refs_0_, f32[16,8,128]{2,1,0:T(8,128)S(1)} %get-tuple-element.8.refs_1_, bf16[8192,512]{1,0:T(8,128)(2,1)S(1)} %copy-done.2), custom_call_target="tpu_custom_call" | custom-call | tf_op jit(solution)/shard_map/pallas_call | solution.py:452
  120.1 0.7 reshape.317
  (90 shorter events, 4.1 us)
Async XLA Ops:
  0.0 43.4 %copy-start = (bf16[8192,2,64]{0,2,1:T(8,128)(2,1)S(1)}, bf16[8192,2,64]{0,2,1:T(8,128)(2,1)}, u32[]{:S(2)}) copy-start(bf16[8192,2,64]{0,2,1:T(8,128)(2,1)} %param.20) | copy-start | bytes 6291460
  0.0 37.2 %copy-start.7 = (f32[512]{0:T(512)S(1)}, f32[512]{0:T(512)}, u32[]{:S(2)}) copy-start(f32[512]{0:T(512)} %param.19) | copy-start | bytes 6148
  37.2 5.4 %copy-start.1 = (bf16[16,8,8192]{2,1,0:T(8,128)(2,1)}, bf16[16,8,8192]{2,1,0:T(8,128)(2,1)S(1)}, u32[]{:S(2)}) copy-start(bf16[16,8,8192]{2,1,0:T(8,128)(2,1)S(1)} %shard_map.154) | copy-start | bytes 6291460
  42.6 0.7 copy-start.10
  43.4 3.5 %copy-start.9 = (s32[32]{0:T(128)S(1)}, s32[32]{0:T(128)}, u32[]{:S(2)}) copy-start(s32[32]{0:T(128)} %param.29) | copy-start | bytes 388
  43.4 4.3 %copy-start.6 = (s32[1,3,16,2]{2,3,1,0:T(2,128)S(1)}, s32[1,3,16,2]{2,3,1,0:T(2,128)}, u32[]{:S(2)}) copy-start(s32[1,3,16,2]{2,3,1,0:T(2,128)} %constant.65.clone.1) | copy-start | bytes 1156
  43.4 5.1 %copy-start.5 = (s32[2]{0:T(128)S(1)}, s32[2]{0:T(128)}, u32[]{:S(2)}) copy-start(s32[2]{0:T(128)} %param.26) | copy-start | bytes 28
  43.4 5.1 %copy-start.8 = (s32[2]{0:T(128)S(1)}, s32[2]{0:T(128)}, u32[]{:S(2)}) copy-start(s32[2]{0:T(128)} %param.25) | copy-start | bytes 28
  52.2 1.2 %copy-start.3 = (bf16[2,256,1024]{2,1,0:T(8,128)(2,1)S(1)}, bf16[2,256,1024]{2,1,0:T(8,128)(2,1)}, u32[]{:S(2)}) copy-start(bf16[2,256,1024]{2,1,0:T(8,128)(2,1)} %param.27) | copy-start | bytes 3145732
  53.4 1.2 %copy-start.4 = (bf16[2,256,1024]{2,1,0:T(8,128)(2,1)S(1)}, bf16[2,256,1024]{2,1,0:T(8,128)(2,1)}, u32[]{:S(2)}) copy-start(bf16[2,256,1024]{2,1,0:T(8,128)(2,1)} %param.28) | copy-start | bytes 3145732
  80.4 3.4 %copy-start.2 = (bf16[8192,512]{1,0:T(8,128)(2,1)S(1)}, bf16[8192,512]{1,0:T(8,128)(2,1)}, u32[]{:S(2)}) copy-start(bf16[8192,512]{1,0:T(8,128)(2,1)} %refs_2_.1) | copy-start | bytes 25165828

commit v4 on v3

--- a/solution.py
+++ b/solution.py
@@ -250,6 +250,15 @@
     return [z + 1 - 2 * (z % 2), (z + 2) % 4, 3 - z]
 
 
+def line(z):
+    near = z + 1 - 2 * (z % 2)
+    return [(near, 3 - z), (2 - z // 2, near), (3 - 3 * (z // 2), near)]
+
+
+def middle(z):
+    return (z + 1) // 2 == 1
+
+
 def greet(z, y, c):
     barrier = pltpu.get_barrier_semaphore()
     others = [at(w, y, c) for w in partners(z)] + [at(z, 1 - y, c), at(z, y, 1 - c)]
@@ -264,7 +273,7 @@
         self.me, self.z, self.y, self.c = place()
         self.sent = []
 
-    def push(self, shard, target, src):
+    def push(self, shard, target, src, only=None):
         copy = pltpu.make_async_remote_copy(
             src_ref=src,
             dst_ref=self.o_ref.at[shard],
@@ -273,8 +282,11 @@
             device_id={"beam": target},
             device_id_type=MESH,
         )
-        copy.start()
-        self.sent.append(copy)
+        if only is None:
+            copy.start()
+        else:
+            pl.when(only)(copy.start)
+        self.sent.append((copy, only))
 
     def arrive(self, shard):
         pltpu.make_async_remote_copy(
@@ -289,19 +301,21 @@
     def run(self, use):
         z, y, c = self.z, self.y, self.c
         over, core = at(z, 1 - y, c), at(z, y, 1 - c)
-        zs = partners(z)
+        hops = line(z)
+        zs = [w for w, _ in hops]
+        inner = middle(z)
+        self.push(self.me, at(3 - z, y, c), self.x_ref, inner)
+        self.push(self.me, at(zs[0], y, c), self.x_ref)
         self.push(self.me, over, self.x_ref)
-        for w in zs[::-1]:
-            self.push(self.me, at(w, y, c), self.x_ref)
         self.push(self.me, core, self.x_ref)
         use(self.me)
-        for k, w in enumerate([z] + zs):
-            if k:
-                shard = at(w, y, c)
-                self.arrive(shard)
-                self.push(shard, over, self.o_ref.at[shard])
-                self.push(shard, core, self.o_ref.at[shard])
-                use(shard)
+        for w, onward in hops:
+            shard = at(w, y, c)
+            self.arrive(shard)
+            self.push(shard, at(onward, y, c), self.o_ref.at[shard], inner)
+            self.push(shard, over, self.o_ref.at[shard])
+            self.push(shard, core, self.o_ref.at[shard])
+            use(shard)
         for w in [z] + zs:
             shard = at(w, 1 - y, c)
             self.arrive(shard)
@@ -312,8 +326,11 @@
                 shard = at(w, v, 1 - c)
                 self.arrive(shard)
                 use(shard)
-        for copy in self.sent:
-            copy.wait_send()
+        for copy, only in self.sent:
+            if only is None:
+                copy.wait_send()
+            else:
+                pl.when(only)(copy.wait_send)
 
 
 def gather_kernel(x_ref, o_ref, send, recv):
@@ -330,7 +347,7 @@
         out_shape=jax.ShapeDtypeStruct((devices,) + x.shape, x.dtype),
         in_specs=[vmem],
         out_specs=vmem,
-        scratch_shapes=[pltpu.SemaphoreType.DMA((15,)), pltpu.SemaphoreType.DMA((16,))],
+        scratch_shapes=[pltpu.SemaphoreType.DMA((19,)), pltpu.SemaphoreType.DMA((16,))],
         compiler_params=pltpu.CompilerParams(
             collective_id=tag, has_side_effects=True, vmem_limit_bytes=32 * 2**20
         ),
@@ -461,7 +478,7 @@
             pltpu.VMEM((depth, cols), jnp.bfloat16),
             pltpu.SemaphoreType.DMA((15, 2)),
             pltpu.SemaphoreType.DMA((15, 2)),
-            pltpu.SemaphoreType.DMA((15,)),
+            pltpu.SemaphoreType.DMA((19,)),
             pltpu.SemaphoreType.DMA((16,)),
             pltpu.SemaphoreType.DMA,
         ],
@@ -499,14 +516,24 @@
             device_id={"beam": core}, device_id_type=MESH,
         ).wait_recv()
 
-    zs = partners(z)
+    inner = middle(z)
+    hops = line(z)
+
+    @pl.when(inner)
+    def _():
+        push(15, me, at(3 - z, y, c), x_ref)
+
+    push(1, me, at(hops[0][0], y, c), x_ref)
     push(0, me, over, x_ref)
-    for k in (2, 1, 0):
-        push(1 + k, me, at(zs[k], y, c), x_ref)
-    push(4, me, core, x_ref)
-    for k, w in enumerate(zs):
+    push(2, me, core, x_ref)
+    for k, (w, onward) in enumerate(hops):
         shard = at(w, y, c)
         arrive(shard)
+
+        @pl.when(inner)
+        def _():
+            push(16 + k, shard, at(onward, y, c), full.at[shard])
+
         push(5 + 2 * k, shard, over, full.at[shard])
         push(6 + 2 * k, shard, core, full.at[shard])
 
@@ -537,7 +564,9 @@
         column[pl.ds(start, ppr), :] = table
 
     def one(i, carry):
-        w = (z // 2 + i % 4 // 2) % 2 * 2 + (z + i) % 2
+        turn = i % 4
+        odd, high = turn % 2, turn // 2
+        w = z + odd * (1 - high) * (hops[0][0] - z) + (1 - odd) * high * (hops[1][0] - z) + odd * high * (hops[2][0] - z)
         v = (y + i // 4) % 2
 
         @pl.when(i < 4)
@@ -598,11 +627,20 @@
         return carry
 
     lax.fori_loop(0, 8, one, 0)
-    for slot in range(15):
+
+    def sent(slot):
         pltpu.make_async_remote_copy(
             src_ref=x_ref, dst_ref=full.at[0], send_sem=send.at[slot], recv_sem=recv.at[0],
             device_id={"beam": core}, device_id_type=MESH,
         ).wait_send()
+
+    for slot in [0, 1, 2] + list(range(5, 15)):
+        sent(slot)
+
+    @pl.when(inner)
+    def _():
+        for slot in range(15, 19):
+            sent(slot)
 
 
 def gather_and_attend(pieces, pk, pv, tk, tv, pok, lok, cs, sn, own, scale, devices, tag):
@@ -619,7 +657,7 @@
         scratch_shapes=[
             pltpu.VMEM((devices,) + pieces.shape, jnp.bfloat16),
             pltpu.VMEM((128, 128), jnp.float32),
-            pltpu.SemaphoreType.DMA((15,)),
+            pltpu.SemaphoreType.DMA((19,)),
             pltpu.SemaphoreType.DMA((16,)),
         ],
         compiler_params=pltpu.CompilerParams(

time: 121 us -> 116 us (0.959)
  Pallas kernels: 88.1 us -> 82.4 us
    pallas_call x1, Pallas kernels: 26.1 us -> 22.3 us  [gather(): pl.pallas_call(gather_kernel, out_shape=jax.ShapeDtypeStruct((devices,) +...]
    pallas_call x1, Pallas kernels: 25.7 us -> 23.8 us  [gather_and_attend(): pl.pallas_call(lambda *refs: attend_kernel(own, scale, *refs), out_shape=...]
where the time goes in v4:
time: 116 us; the launch traced here: 115 us
  Pallas kernels  82.4 us (71%)
  local copies, waits for them, and re-layouts  15.8 us (14%)
  other arithmetic  8.88 us (8%)
  matrix products  7.75 us (7%)
    pallas_call x1, Pallas kernels, merge_and_project(): pl.pallas_call(lambda *refs: merge_kernel(heads, rows, *refs), out_shape=...  36.3 us
    pallas_call x1, Pallas kernels, gather_and_attend(): pl.pallas_call(lambda *refs: attend_kernel(own, scale, *refs), out_shape=...  23.8 us
    pallas_call x1, Pallas kernels, gather(): pl.pallas_call(gather_kernel, out_shape=jax.ShapeDtypeStruct((devices,) +...  22.3 us
    unnamed x25, local copies, waits for them, and re-layouts  5.88 us
    dot_general x1, matrix products, local(): jnp.dot(normed, q_weight, preferred_element_type=jnp.float32) + q_bias  5.4 us
    add x2, other arithmetic, lineage_tables(): pos_steps.append(base + lens + step)  2.7 us
    dot_general x1, matrix products, local(): jnp.dot(normed, kv_weight.reshape(width, 2 * kv_cols), preferred_element_...  2.35 us

profile of v4, /device:TPU:0, one launch (start us, length us, event | category | flops | bytes accessed | tf_op | source)
XLA Modules:
  0.0 115.1 jit_solution(18052128828480990570)
XLA Ops:
  0.0 0.9 slice_bitcast_fusion
  0.9 0.2 select_reduce_fusion.8
  1.1 0.2 select_reduce_fusion.2
  1.2 0.9 select_reduce_fusion.1
  2.2 1.3 %fusion.51 = (s32[1]{0:T(128)}, s32[1]{0:T(128)}) fusion(s32[2]{0:T(128)} %param.26), kind=kLoop, calls=%fused_computation.102 | loop fusion | bytes 16 | tf_op jit(solution)/shard_map/gather | solution.py:675
  3.5 1.3 %add_add_fusion.1 = (s32[32]{0:T(128)S(1)}, s32[32]{0:T(128)S(1)}) fusion(s32[32]{0:T(128)S(1)} %get-tuple-element.12, s32[]{:T(128)} %bitcast.3, s32[]{:T(128)} %bitcast.2, s32[32]{0:T(128)S(1)} %get-tuple-element.13), kind=kLoop, calls=%fused_computation.94 | loop fusion | flops 512 | bytes 520 | tf_op jit(solution)/shard_map/add | solution.py:683
  5.2 0.8 select_reduce_fusion.3
  6.0 1.4 %add_add_fusion = s32[32]{0:T(128)S(1)} fusion(s32[32]{0:T(128)S(1)} %select_reduce_fusion.3, s32[]{:T(128)} %bitcast.3, s32[]{:T(128)} %bitcast.2), kind=kLoop, calls=%fused_computation.92 | loop fusion | flops 480 | bytes 264 | tf_op jit(solution)/shard_map/add | solution.py:683
  7.7 0.1 convert_element_type.70
  7.8 0.9 fusion.41
  8.7 1.1 fusion.22
  9.8 1.1 fusion.24
  11.0 22.3 %shard_map.154 = bf16[16,8,8192]{2,1,0:T(8,128)(2,1)S(1)} custom-call(bf16[8,8192]{1,0:T(8,128)(2,1)S(1)} %pad.18.x_ref), custom_call_target="tpu_custom_call" | custom-call | tf_op jit(solution)/shard_map/pallas_call | solution.py:345
  33.3 5.4 %fusion.10 = bf16[16,8,512]{2,1,0:T(8,128)(2,1)S(1)} fusion(bf16[8192,512]{1,0:T(8,128)(2,1)} %param.18, bf16[16,8,8192]{2,1,0:T(8,128)(2,1)S(1)} %shard_map.154, f32[512]{0:T(512)S(1)} %copy-done.7), kind=kOutput, calls=%fused_computation.8 | convolution fusion | flops 1073872896 | bytes 10618880 | tf_op jit(solution)/shard_map/dot_general | solution.py:741
  39.6 2.3 %fusion.19 = bf16[16,8,128]{2,1,0:T(8,128)(2,1)S(1)} fusion(bf16[8192,128]{0,1:T(8,128)(2,1)S(1)} %bitcast.79, bf16[16,8,8192]{2,1,0:T(8,128)(2,1)} %copy-done.1, f32[128]{0:T(128)S(1)} %add.187), kind=kOutput, calls=%fused_computation.11 | convolution fusion | flops 268468224 | bytes 4227584 | tf_op jit(solution)/shard_map/dot_general | solution.py:742
  42.6 0.1 reshape.314
  44.7 1.8 %gather_fusion = bf16[2,128,1024]{2,1,0:T(8,128)(2,1)S(1)} fusion(bf16[4,128,1024]{2,1,0:T(8,128)(2,1)} %param.23, s32[1024]{0:T(1024)S(1)} %pad_clamp_fusion), kind=kCustom, calls=%fused_computation | custom fusion | bytes 1048584 | tf_op jit(solution)/shard_map/jit(_take)/gather | solution.py:771
  46.5 1.8 %gather_fusion.1 = bf16[2,128,1024]{2,1,0:T(8,128)(2,1)S(1)} fusion(bf16[4,128,1024]{2,1,0:T(8,128)(2,1)} %param.24, s32[1024]{0:T(1024)S(1)} %pad_clamp_fusion), kind=kCustom, calls=%fused_computation.1 | custom fusion | bytes 1048584 | tf_op jit(solution)/shard_map/jit(_take)/gather | solution.py:772
  48.4 1.2 %copy-done.3 = bf16[2,256,1024]{2,1,0:T(8,128)(2,1)S(1)} copy-done((bf16[2,256,1024]{2,1,0:T(8,128)(2,1)S(1)}, bf16[2,256,1024]{2,1,0:T(8,128)(2,1)}, u32[]{:S(2)}) %copy-start.3) | copy-done | bytes 1048600
  49.6 1.2 %copy-done.4 = bf16[2,256,1024]{2,1,0:T(8,128)(2,1)S(1)} copy-done((bf16[2,256,1024]{2,1,0:T(8,128)(2,1)S(1)}, bf16[2,256,1024]{2,1,0:T(8,128)(2,1)}, u32[]{:S(2)}) %copy-start.4) | copy-done | bytes 1048600
  50.8 23.8 %shard_map.155 = (bf16[16,384,128]{2,1,0:T(8,128)(2,1)S(1)}, f32[16,8,128]{2,1,0:T(8,128)S(1)}) custom-call(bf16[5,96,128]{2,1,0:T(8,128)(2,1)S(1)} %constant_dynamic-update-slice_fusion.refs_0_, bf16[2,128,1024]{2,1,0:T(8,128)(2,1)S(1)} %gather_fusion, bf16[2,128,1024]{2,1,0:T(8,128)(2,1)S(1)} %gather_fusion.1, bf16[512,1024]{1,0:T(8,128)(2,1)S(1)} %bitcast.80, ...), custom_call_target="tpu_custom_call" | custom-call | tf_op jit(solution)/shard_map/pallas_call | solution.py:649
  74.6 3.4 %copy-done.2 = bf16[8192,512]{1,0:T(8,128)(2,1)S(1)} copy-done((bf16[8192,512]{1,0:T(8,128)(2,1)S(1)}, bf16[8192,512]{1,0:T(8,128)(2,1)}, u32[]{:S(2)}) %copy-start.2) | copy-done | bytes 8388632
  78.0 36.3 %shard_map.156 = bf16[96,512]{1,0:T(8,128)(2,1)S(1)} custom-call(bf16[16,384,128]{2,1,0:T(8,128)(2,1)S(1)} %get-tuple-element.7.refs_0_, f32[16,8,128]{2,1,0:T(8,128)S(1)} %get-tuple-element.8.refs_1_, bf16[8192,512]{1,0:T(8,128)(2,1)S(1)} %copy-done.2), custom_call_target="tpu_custom_call" | custom-call | tf_op jit(solution)/shard_map/pallas_call | solution.py:469
  114.5 0.7 reshape.317
  (90 shorter events, 4.1 us)
Async XLA Ops:
  0.0 39.6 %copy-start = (bf16[8192,2,64]{0,2,1:T(8,128)(2,1)S(1)}, bf16[8192,2,64]{0,2,1:T(8,128)(2,1)}, u32[]{:S(2)}) copy-start(bf16[8192,2,64]{0,2,1:T(8,128)(2,1)} %param.20) | copy-start | bytes 6291460
  0.0 33.3 %copy-start.7 = (f32[512]{0:T(512)S(1)}, f32[512]{0:T(512)}, u32[]{:S(2)}) copy-start(f32[512]{0:T(512)} %param.19) | copy-start | bytes 6148
  33.3 5.4 %copy-start.1 = (bf16[16,8,8192]{2,1,0:T(8,128)(2,1)}, bf16[16,8,8192]{2,1,0:T(8,128)(2,1)S(1)}, u32[]{:S(2)}) copy-start(bf16[16,8,8192]{2,1,0:T(8,128)(2,1)S(1)} %shard_map.154) | copy-start | bytes 6291460
  38.7 0.7 copy-start.10
  39.6 3.5 %copy-start.9 = (s32[32]{0:T(128)S(1)}, s32[32]{0:T(128)}, u32[]{:S(2)}) copy-start(s32[32]{0:T(128)} %param.29) | copy-start | bytes 388
  39.6 4.3 %copy-start.6 = (s32[1,3,16,2]{2,3,1,0:T(2,128)S(1)}, s32[1,3,16,2]{2,3,1,0:T(2,128)}, u32[]{:S(2)}) copy-start(s32[1,3,16,2]{2,3,1,0:T(2,128)} %constant.65.clone.1) | copy-start | bytes 1156
  39.6 5.1 %copy-start.5 = (s32[2]{0:T(128)S(1)}, s32[2]{0:T(128)}, u32[]{:S(2)}) copy-start(s32[2]{0:T(128)} %param.26) | copy-start | bytes 28
  39.6 5.2 %copy-start.8 = (s32[2]{0:T(128)S(1)}, s32[2]{0:T(128)}, u32[]{:S(2)}) copy-start(s32[2]{0:T(128)} %param.25) | copy-start | bytes 28
  48.4 1.2 %copy-start.3 = (bf16[2,256,1024]{2,1,0:T(8,128)(2,1)S(1)}, bf16[2,256,1024]{2,1,0:T(8,128)(2,1)}, u32[]{:S(2)}) copy-start(bf16[2,256,1024]{2,1,0:T(8,128)(2,1)} %param.27) | copy-start | bytes 3145732
  49.6 1.2 %copy-start.4 = (bf16[2,256,1024]{2,1,0:T(8,128)(2,1)S(1)}, bf16[2,256,1024]{2,1,0:T(8,128)(2,1)}, u32[]{:S(2)}) copy-start(bf16[2,256,1024]{2,1,0:T(8,128)(2,1)} %param.28) | copy-start | bytes 3145732
  74.6 3.4 %copy-start.2 = (bf16[8192,512]{1,0:T(8,128)(2,1)S(1)}, bf16[8192,512]{1,0:T(8,128)(2,1)}, u32[]{:S(2)}) copy-start(bf16[8192,512]{1,0:T(8,128)(2,1)} %refs_2_.1) | copy-start | bytes 25165828

commit v5 on v4

--- a/solution.py
+++ b/solution.py
@@ -469,7 +469,7 @@
     return pl.pallas_call(
         lambda *refs: merge_kernel(heads, rows, *refs),
         out_shape=jax.ShapeDtypeStruct((rows, cols), jnp.bfloat16),
-        in_specs=[vmem, vmem, pl.BlockSpec(memory_space=pl.ANY)],
+        in_specs=[vmem, vmem, pl.BlockSpec(memory_space=pltpu.HBM)],
         out_specs=vmem,
         scratch_shapes=[
             bf(8), fl(8), bf(8), fl(8), bf(4), fl(4), bf(4), fl(4), bf(3), fl(3),
@@ -489,7 +489,7 @@
 
 
 def attend_kernel(
-    own, scale, x_ref, pk_ref, pv_ref, tk_ref, tv_ref, pok_ref, lok_ref, cs_ref, sn_ref,
+    own, scale, x_ref, oh_ref, pk_ref, pv_ref, tk_ref, tv_ref, pok_ref, lok_ref, cs_ref, sn_ref,
     num_ref, st_ref, full, column, send, recv,
 ):
     me, z, y, c = place()
@@ -587,8 +587,14 @@
         key = jnp.concatenate([key.astype(jnp.bfloat16), blank], 0)
         value = jnp.concatenate([value.astype(jnp.bfloat16), blank], 0)
 
+        def chosen(ref, prompt):
+            entry = ref[0, :, cols].astype(jnp.float32) * oh_ref[prompt, 0][:1]
+            for j in range(1, ref.shape[0]):
+                entry = entry + ref[j, :, cols].astype(jnp.float32) * oh_ref[prompt, j][:1]
+            return entry.astype(jnp.bfloat16)
+
         def prefix(prompt, q):
-            keys = pk_ref[prompt, :, cols]
+            keys = chosen(pk_ref, prompt)
             s = lax.dot_general(q, keys, contract, preferred_element_type=jnp.float32) * scale
             ok = pok_ref[prompt][:1] > 0.0
             return jnp.where(ok, s, NEG), ok
@@ -597,7 +603,7 @@
         s, ok = prefix(1 - my_prompt, q)
         top = jnp.max(s, axis=1, keepdims=True)
         e = jnp.where(ok, jnp.exp(s - top), 0.0)
-        num = jnp.dot(e.astype(jnp.bfloat16), pv_ref[1 - my_prompt, :, cols], preferred_element_type=jnp.float32)
+        num = jnp.dot(e.astype(jnp.bfloat16), chosen(pv_ref, 1 - my_prompt), preferred_element_type=jnp.float32)
         write(k, 1 - my_prompt, num, top, jnp.sum(e, axis=1, keepdims=True))
 
         q = queries(k, my_prompt)
@@ -616,7 +622,7 @@
         le = jnp.where(lok, jnp.exp(ls - top), 0.0)
         total = jnp.sum(e, axis=1, keepdims=True) + jnp.sum(le, axis=1, keepdims=True)
         le = le.astype(jnp.bfloat16)
-        num = jnp.dot(e.astype(jnp.bfloat16), pv_ref[my_prompt, :, cols], preferred_element_type=jnp.float32)
+        num = jnp.dot(e.astype(jnp.bfloat16), chosen(pv_ref, my_prompt), preferred_element_type=jnp.float32)
         num = num + jnp.dot(le[:, :tail], tv_ref[:, cols], preferred_element_type=jnp.float32)
         num = num + jnp.dot(le[:, tail:], value, preferred_element_type=jnp.float32)
         write(k, my_prompt, num, top, total)
@@ -643,7 +649,7 @@
             sent(slot)
 
 
-def gather_and_attend(pieces, pk, pv, tk, tv, pok, lok, cs, sn, own, scale, devices, tag):
+def gather_and_attend(pieces, oh, pk, pv, tk, tv, pok, lok, cs, sn, own, scale, devices, tag):
     vmem = pl.BlockSpec(memory_space=pltpu.VMEM)
     heads, rows = pieces.shape[0] - 1, pieces.shape[1]
     return pl.pallas_call(
@@ -652,7 +658,7 @@
             jax.ShapeDtypeStruct((devices, heads * rows, HEAD_DIM), jnp.bfloat16),
             jax.ShapeDtypeStruct((devices, 2 * heads, 128), jnp.float32),
         ],
-        in_specs=[vmem] * 9,
+        in_specs=[vmem] * 10,
         out_specs=[vmem, vmem],
         scratch_shapes=[
             pltpu.VMEM((devices,) + pieces.shape, jnp.bfloat16),
@@ -663,7 +669,7 @@
         compiler_params=pltpu.CompilerParams(
             collective_id=tag, has_side_effects=True, vmem_limit_bytes=40 * 2**20
         ),
-    )(pieces, pk, pv, tk, tv, pok, lok, cs, sn)
+    )(pieces, oh, pk, pv, tk, tv, pok, lok, cs, sn)
 
 
 def lineage_tables(parents, prefix_lens, tail_lens, rows_per_chip, devices):
@@ -766,10 +772,12 @@
     pok = jnp.broadcast_to(pok.astype(jnp.float32)[:, None], (prompts, 8, slab))
     my_cos = jnp.pad(lax.dynamic_slice_in_dim(cosine2, me * own, own, 0), ((0, 16 - own), (0, 0)))
     my_sin = jnp.pad(lax.dynamic_slice_in_dim(sine2, me * own, own, 0), ((0, 16 - own), (0, 0)))
+    pool_hot = prefix_index[:, None] == jnp.arange(prefix_key_cache.shape[0], dtype=jnp.int32)[None, :]
     num, stats = gather_and_attend(
         jnp.stack(pieces, 0),
-        jnp.take(prefix_key_cache, prefix_index, axis=0, mode="clip"),
-        jnp.take(prefix_value_cache, prefix_index, axis=0, mode="clip"),
+        jnp.broadcast_to(pool_hot.astype(jnp.float32)[:, :, None, None], pool_hot.shape + (8, HEAD_DIM)),
+        prefix_key_cache,
+        prefix_value_cache,
         tail_key_cache.reshape(rpc * tail, -1),
         tail_value_cache.reshape(rpc * tail, -1),
         pok, lok, my_cos, my_sin, own, score_scale, devices, 1,

time: 116 us -> 117 us (level)
  other arithmetic: 8.88 us -> 11.8 us
  matrix products: 7.75 us -> 6.01 us
    gather x2 -> x0, local copies, waits for them, and re-layouts: 3.61 us -> none  [the longest x1 1.81 us: local(): jnp.take(prefix_value_cache, prefix_index, axis=0, mode='clip')]
    dot_general x1, matrix products: 2.35 us -> 0.72 us  [local(): jnp.dot(normed, kv_weight.reshape(width, 2 * kv_cols), preferred_element_...]
    unnamed x25 -> x21, local copies, waits for them, and re-layouts: 5.88 us -> 7.03 us
where the time goes in v5:
time: 117 us
  Pallas kernels  82.3 us (70%)
  local copies, waits for them, and re-layouts  16.3 us (14%)
  other arithmetic  11.8 us (10%)
  matrix products  6.01 us (5%)
    pallas_call x1, Pallas kernels, merge_and_project(): pl.pallas_call(lambda *refs: merge_kernel(heads, rows, *refs), out_shape=...  36.3 us
    pallas_call x1, Pallas kernels, gather_and_attend(): pl.pallas_call(lambda *refs: attend_kernel(own, scale, *refs), out_shape=...  23.8 us
    pallas_call x1, Pallas kernels, gather(): pl.pallas_call(gather_kernel, out_shape=jax.ShapeDtypeStruct((devices,) +...  22.2 us
    unnamed x21, local copies, waits for them, and re-layouts  7.03 us
    dot_general x1, matrix products, local(): jnp.dot(normed, q_weight, preferred_element_type=jnp.float32) + q_bias  5.29 us
    add x2, other arithmetic, lineage_tables(): pos_steps.append(base + lens + step)  2.7 us

profile of v5, /device:TPU:0, one launch (start us, length us, event | category | flops | bytes accessed | tf_op | source)
XLA Modules:
  0.0 116.7 jit_solution(9806338484547251361)
XLA Ops:
  0.0 0.9 dynamic_slice.16
  0.9 0.7 copy-done
  1.6 0.8 add.187
  2.4 0.7 compare_convert_fusion
  3.1 0.7 compare_convert_fusion.1
  3.8 1.3 %fusion.51 = (s32[1]{0:T(128)}, s32[1]{0:T(128)}) fusion(s32[2]{0:T(128)} %param.26), kind=kLoop, calls=%fused_computation.100 | loop fusion | bytes 16 | tf_op jit(solution)/shard_map/gather | solution.py:681
  5.2 0.8 slice_bitcast_fusion
  6.4 1.1 fusion.22
  7.7 0.9 select_reduce_fusion.1
  8.6 0.8 select_reduce_fusion.3
  9.4 1.4 %add_add_fusion = s32[32]{0:T(128)S(1)} fusion(s32[32]{0:T(128)S(1)} %select_reduce_fusion.3, s32[]{:T(128)} %bitcast.3, s32[]{:T(128)} %bitcast.2), kind=kLoop, calls=%fused_computation.90 | loop fusion | flops 480 | bytes 264 | tf_op jit(solution)/shard_map/add | solution.py:689
  10.8 1.3 %add_add_fusion.1 = (s32[32]{0:T(128)S(1)}, s32[32]{0:T(128)S(1)}) fusion(s32[32]{0:T(128)S(1)} %get-tuple-element.12, s32[]{:T(128)} %bitcast.3, s32[]{:T(128)} %bitcast.2, s32[32]{0:T(128)S(1)} %get-tuple-element.13), kind=kLoop, calls=%fused_computation.92 | loop fusion | flops 512 | bytes 520 | tf_op jit(solution)/shard_map/add | solution.py:689
  13.7 0.8 add_bitcast_fusion
  15.8 1.1 fusion.24
  16.9 0.9 fusion.41
  18.5 22.2 %shard_map.154 = bf16[16,8,8192]{2,1,0:T(8,128)(2,1)S(1)} custom-call(bf16[8,8192]{1,0:T(8,128)(2,1)S(1)} %pad.18.x_ref), custom_call_target="tpu_custom_call" | custom-call | tf_op jit(solution)/shard_map/pallas_call | solution.py:345
  41.4 5.3 %fusion.10 = bf16[16,8,512]{2,1,0:T(8,128)(2,1)} fusion(bf16[8192,512]{1,0:T(8,128)(2,1)} %param.18, bf16[16,8,8192]{2,1,0:T(8,128)(2,1)S(1)} %shard_map.154, f32[512]{0:T(512)S(1)} %copy-done.8), kind=kOutput, calls=%fused_computation.6 | convolution fusion | flops 1073872896 | bytes 10618880 | tf_op jit(solution)/shard_map/dot_general | solution.py:747
  46.7 1.0 reshape.331
  48.6 1.0 fusion.40
  50.0 1.2 %copy-done.4 = bf16[2,256,1024]{2,1,0:T(8,128)(2,1)S(1)} copy-done((bf16[2,256,1024]{2,1,0:T(8,128)(2,1)S(1)}, bf16[2,256,1024]{2,1,0:T(8,128)(2,1)}, u32[]{:S(2)}) %copy-start.4) | copy-done | bytes 1048600
  51.2 1.2 %copy-done.5 = bf16[2,256,1024]{2,1,0:T(8,128)(2,1)S(1)} copy-done((bf16[2,256,1024]{2,1,0:T(8,128)(2,1)S(1)}, bf16[2,256,1024]{2,1,0:T(8,128)(2,1)}, u32[]{:S(2)}) %copy-start.5) | copy-done | bytes 1048600
  52.4 23.8 %shard_map.155 = (bf16[16,384,128]{2,1,0:T(8,128)(2,1)S(1)}, f32[16,8,128]{2,1,0:T(8,128)S(1)}) custom-call(bf16[5,96,128]{2,1,0:T(8,128)(2,1)S(1)} %constant_dynamic-update-slice_fusion.refs_0_, f32[2,4,8,128]{3,2,1,0:T(8,128)S(1)} %broadcast_in_dim.101.refs_1_, bf16[4,128,1024]{2,1,0:T(8,128)(2,1)S(1)} %copy-done.2, bf16[4,128,1024]{2,1,0:T(8,128)(2,1)S(1)} %copy-done.3, ...), custom_call_target="tpu_custom_call" | custom-call | tf_op jit(solution)/shard_map/pallas_call | solution.py:655
  76.2 3.4 %copy-done.1 = bf16[8192,512]{1,0:T(8,128)(2,1)S(1)} copy-done((bf16[8192,512]{1,0:T(8,128)(2,1)S(1)}, bf16[8192,512]{1,0:T(8,128)(2,1)}, u32[]{:S(2)}) %copy-start.1) | copy-done | bytes 8388632
  79.6 36.3 %shard_map.156 = bf16[96,512]{1,0:T(8,128)(2,1)S(1)} custom-call(bf16[16,384,128]{2,1,0:T(8,128)(2,1)S(1)} %get-tuple-element.7.refs_0_, f32[16,8,128]{2,1,0:T(8,128)S(1)} %get-tuple-element.8.refs_1_, bf16[8192,512]{1,0:T(8,128)(2,1)S(1)} %copy-done.1), custom_call_target="tpu_custom_call" | custom-call | tf_op jit(solution)/shard_map/pallas_call | solution.py:469
  (85 shorter events, 6.8 us)
Async XLA Ops:
  0.0 1.6 %copy-start = (bf16[8192,2,64]{0,2,1:T(8,128)(2,1)S(1)}, bf16[8192,2,64]{0,2,1:T(8,128)(2,1)}, u32[]{:S(2)}) copy-start(bf16[8192,2,64]{0,2,1:T(8,128)(2,1)} %param.20) | copy-start | bytes 6291460
  17.9 0.6 copy-start.6
  40.7 0.7 copy-start.8
  46.7 3.2 %copy-start.2 = (bf16[4,128,1024]{2,1,0:T(8,128)(2,1)S(1)}, bf16[4,128,1024]{2,1,0:T(8,128)(2,1)}, u32[]{:S(2)}) copy-start(bf16[4,128,1024]{2,1,0:T(8,128)(2,1)} %refs_2_.2) | copy-start | bytes 3145732
  48.4 1.6 %copy-start.7 = (bf16[1,96,128]{2,1,0:T(8,128)(2,1)S(1)}, bf16[1,96,128]{2,1,0:T(8,128)(2,1)}, u32[]{:S(2)}) copy-start(bf16[1,96,128]{2,1,0:T(8,128)(2,1)} %stack_reshape.3) | copy-start | bytes 73732
  48.4 1.6 %copy-start.3 = (bf16[4,128,1024]{2,1,0:T(8,128)(2,1)S(1)}, bf16[4,128,1024]{2,1,0:T(8,128)(2,1)}, u32[]{:S(2)}) copy-start(bf16[4,128,1024]{2,1,0:T(8,128)(2,1)} %refs_3_.1) | copy-start | bytes 3145732
  50.0 1.2 %copy-start.4 = (bf16[2,256,1024]{2,1,0:T(8,128)(2,1)S(1)}, bf16[2,256,1024]{2,1,0:T(8,128)(2,1)}, u32[]{:S(2)}) copy-start(bf16[2,256,1024]{2,1,0:T(8,128)(2,1)} %param.27) | copy-start | bytes 3145732
  51.2 1.2 %copy-start.5 = (bf16[2,256,1024]{2,1,0:T(8,128)(2,1)S(1)}, bf16[2,256,1024]{2,1,0:T(8,128)(2,1)}, u32[]{:S(2)}) copy-start(bf16[2,256,1024]{2,1,0:T(8,128)(2,1)} %param.28) | copy-start | bytes 3145732
  76.2 3.4 %copy-start.1 = (bf16[8192,512]{1,0:T(8,128)(2,1)S(1)}, bf16[8192,512]{1,0:T(8,128)(2,1)}, u32[]{:S(2)}) copy-start(bf16[8192,512]{1,0:T(8,128)(2,1)} %refs_2_.3) | copy-start | bytes 25165828
